TPU v7x, 32 devices: a whole 2x2x4 slice. The times are simulated.
32 devices in a mesh: group: 2 (over x), row: 8 (over z, y), tp: 2 (over core).
Axes of the slice: x: 2, y: 2, z: 4, core: 2. Of those that a mesh axis runs over, the one named last changes fastest.
Arguments:
- prompt_latent: bfloat16 [16, 16, 128, 576], P(('group', 'row'), None, 'tp'), parts along dimension 0, may hold values from -6 to 6
- row_cache: bfloat16 [32, 256, 576], P(('group', 'row')), parts along dimension 0, may hold values from -24 to 24
- queries: bfloat16 [4, 32, 128, 576], P(None, ('group', 'row'), 'tp'), parts along dimension 1, may hold values from -80 to 80
- new_latent: bfloat16 [4, 32, 576], P(None, ('group', 'row')), parts along dimension 1, may hold values from -12 to 12
- prompt_len: int32 [32], P('group'), parts along dimension 0, may hold values from 1 to 1024, 12288 in all
- assign: int32 [32], P('group'), parts along dimension 0, may hold values from 0 to 15, as said below
- row_ctx: int32 [32], P(('group', 'row')), parts along dimension 0, may hold values from 2 to 256
Outputs:
- attended: bfloat16 [4, 32, 128, 512], P(None, ('group', 'row'), 'tp'), parts along dimension 1
There are 2 independent parts, one for each index of `group`. A program takes and returns all parts, laid end to end along the dimension named above; each array names one. Nothing has to cross between parts.
Inputs may be any that keep to these rules, and one draw needn't show every extreme that they name: `prompt_len`: latents at positions from a prompt's length on are not part of that prompt. Decode row r continues prompt assign[r]; every prompt goes to exactly one row. Prompt p belongs to prompt group p // 16; the rows of one index of row take at most 2 prompts of any one prompt group. Row r's cached latents are its first row_ctx[r] positions.
All inputs are finite; a program needn't handle non-finite values.
Results may differ from a plain program's by a relative error of at most 0.0044.
Values may be sent and summed in bfloat16 or wider, within the bound.
No kernel may reach another device: no remote copies, remote signals or barrier semaphores. Data moves between devices by JAX's collectives and lax.ppermute only.
A program may use at most 128 MiB of HBM per device.

v0:
```python
import jax
import jax.numpy as jnp
from jax import lax
from jax.sharding import PartitionSpec as P

KV_RANK = 512
ROPE_DIM = 64
NOPE_DIM = 128
SPR = 8


def shards(prompt_latent, row_cache, queries, new_latent, prompt_len, assign, row_ctx):
    row_count = lax.axis_size("row")
    pair_count = lax.axis_size("tp")
    row_place = lax.axis_index("row")
    rows_here = row_cache.shape[0]
    group_rows = prompt_latent.shape[1]
    piece_len = prompt_latent.shape[2]
    latent_width = prompt_latent.shape[3]
    full_len = piece_len * SPR * pair_count
    most_slots = min(rows_here, max(2, 2 * rows_here * SPR // row_count))
    home_group = row_place // SPR
    dest_prompt = assign.reshape(row_count, rows_here)
    in_group = dest_prompt // group_rows == home_group
    rank = jnp.cumsum(in_group.astype(jnp.int32), axis=1) - 1
    slot_ids = jnp.arange(most_slots, dtype=jnp.int32)
    picked = in_group[:, :, None] & (rank[:, :, None] == slot_ids[None, None, :])
    local_id = dest_prompt - home_group * group_rows
    source_index = jnp.sum(jnp.where(picked, local_id[:, :, None], 0), axis=1)
    filled = jnp.any(picked, axis=1).reshape(-1)
    owned = lax.dynamic_slice_in_dim(assign, row_place * rows_here, rows_here)
    owned_group = owned // group_rows
    row_ids = jnp.arange(rows_here, dtype=jnp.int32)
    same_before = (owned_group[:, None] == owned_group[None, :]) & (
        row_ids[None, :] < row_ids[:, None]
    )
    own_rank = jnp.sum(same_before.astype(jnp.int32), axis=1)
    block_ids = jnp.arange(SPR, dtype=jnp.int32)
    fetch_index = (
        (owned_group[:, None] * SPR + block_ids[None, :]) * most_slots + own_rank[:, None]
    ).reshape(-1)
    local = prompt_latent[0]
    rows_taken = jnp.take(local, source_index.reshape(-1), axis=0)
    rows_taken = jnp.where(filled[:, None, None], rows_taken, jnp.zeros_like(rows_taken))
    moved = lax.all_to_all(
        rows_taken.reshape((row_count, most_slots) + local.shape[1:]),
        "row",
        split_axis=0,
        concat_axis=0,
        tiled=True,
    )
    flat = moved.reshape(row_count * most_slots, piece_len, latent_width)
    mine = jnp.take(flat, fetch_index, axis=0).reshape(rows_here, SPR, 1, piece_len, latent_width)
    paired = lax.all_gather(mine, "tp", axis=2, tiled=True)
    latents = paired.reshape(rows_here, full_len, latent_width)
    live_len = jnp.take(prompt_len, owned)
    scale_factor = (NOPE_DIM + ROPE_DIM) ** (-0.5)
    steps_count = queries.shape[0]
    cache_len = row_cache.shape[1]
    cache_scores = (
        jnp.einsum("srhc,rkc->rshk", queries, row_cache, preferred_element_type=jnp.float32)
        * scale_factor
    )
    cache_live = jnp.arange(cache_len, dtype=jnp.int32)[None, :] < row_ctx[:, None]
    cache_scores = jnp.where(cache_live[:, None, None, :], cache_scores, -jnp.inf)
    fresh_scores = (
        jnp.einsum("srhc,jrc->rshj", queries, new_latent, preferred_element_type=jnp.float32)
        * scale_factor
    )
    step_ids = jnp.arange(steps_count, dtype=jnp.int32)
    causal = step_ids[None, :] <= step_ids[:, None]
    fresh_scores = jnp.where(causal[None, :, None, :], fresh_scores, -jnp.inf)
    prompt_live = jnp.arange(full_len, dtype=jnp.int32)[None, :] < live_len[:, None]
    prompt_scores = (
        jnp.einsum("srhc,rkc->rshk", queries, latents, preferred_element_type=jnp.float32)
        * scale_factor
    )
    prompt_scores = jnp.where(prompt_live[:, None, None, :], prompt_scores, -jnp.inf)
    row_top = jnp.maximum(
        jnp.max(prompt_scores, axis=3, keepdims=True),
        jnp.maximum(
            jnp.max(cache_scores, axis=3, keepdims=True),
            jnp.max(fresh_scores, axis=3, keepdims=True),
        ),
    )
    prompt_exp = jnp.exp(prompt_scores - row_top)
    cache_exp = jnp.exp(cache_scores - row_top)
    fresh_exp = jnp.exp(fresh_scores - row_top)
    denominator = (
        jnp.sum(prompt_exp, axis=3, keepdims=True)
        + jnp.sum(cache_exp, axis=3, keepdims=True)
        + jnp.sum(fresh_exp, axis=3, keepdims=True)
    )
    prompt_probs = (prompt_exp / denominator).astype(jnp.bfloat16)
    cache_probs = (cache_exp / denominator).astype(jnp.bfloat16)
    fresh_probs = (fresh_exp / denominator).astype(jnp.bfloat16)
    cache_out = jnp.einsum(
        "rshk,rkc->srhc", cache_probs, row_cache[:, :, :KV_RANK], preferred_element_type=jnp.float32
    )
    fresh_out = jnp.einsum(
        "rshj,jrc->srhc",
        fresh_probs,
        new_latent[:, :, :KV_RANK],
        preferred_element_type=jnp.float32,
    )
    prompt_out = jnp.einsum(
        "rshk,rkc->srhc", prompt_probs, latents[:, :, :KV_RANK], preferred_element_type=jnp.float32
    )
    return (prompt_out + cache_out + fresh_out).astype(jnp.bfloat16)


def solution(mesh):
    return jax.shard_map(
        shards,
        mesh=mesh,
        in_specs=(
            P(("group", "row"), None, "tp", None),
            P(("group", "row"), None, None),
            P(None, ("group", "row"), "tp", None),
            P(None, ("group", "row"), None),
            P("group"),
            P("group"),
            P(("group", "row")),
        ),
        out_specs=P(None, ("group", "row"), "tp", None),
        check_vma=False,
    )
```

profile of v0, /device:TPU:0, one launch (start us, length us, event | category | flops | bytes accessed | tf_op | source)
XLA Modules:
  0.0 77.7 jit_solution(2219437456405683239)
XLA Ops:
  6.5 0.8 %reshape.181 = s32[8,2]{1,0:T(8,128)S(1)} reshape(s32[16]{0:T(128)} %param.14) | data formatting | bytes 128 | tf_op jit(solution)/shard_map/reshape | solution.py:23
  7.4 0.2 reduce_window_sum.11
  7.6 0.1 copy.34
  8.1 0.1 copy.36
  8.1 0.1 broadcast_in_dim.100
  8.2 0.8 %gather_fusion.1 = bf16[16,64,576]{2,1,0:T(8,128)(2,1)S(1)} fusion(bf16[16,64,576]{2,1,0:T(8,128)(2,1)S(1)} %bitcast.68, s32[1024]{0:T(1024)S(1)} %pad_clamp_fusion.2), kind=kCustom, calls=%fused_computation.clone | custom fusion | bytes 2359360 | tf_op jit(solution)/shard_map/jit(_take)/gather | solution.py:43
  9.0 1.4 %select_select_fusion = bf16[16,64,576]{2,1,0:T(8,128)(2,1)} fusion(bf16[16,64,576]{2,1,0:T(8,128)(2,1)S(1)} %gather_fusion.1, pred[16]{0:T(512)(128)(4,1)S(1)} %compare_and_fusion.2, pred[16]{0:T(512)(128)(4,1)S(1)} %broadcast_in_dim.100), kind=kLoop, calls=%fused_computation.16 | loop fusion | flops 1179648 | bytes 2359328 | tf_op jit(solution)/shard_map/jit(_where)/select_n | solution.py:44
  10.4 7.3 %all-to-all-start = ((bf16[8,2,64,576]{3,2,1,0:T(8,128)(2,1)}), bf16[8,2,64,576]{3,2,1,0:T(8,128)(2,1)S(1)}, u32[]{:S(2)}, u32[]{:S(2)}) async-start(bf16[8,2,64,576]{3,2,1,0:T(8,128)(2,1)} %bitcast.70), calls=%async_computation | async-start | bytes 2621440 | tf_op jit(solution)/shard_map/all_to_all | solution.py:45
  17.9 0.2 fusion.32
  18.2 30.9 %all-to-all-done = bf16[8,2,64,576]{3,2,1,0:T(8,128)(2,1)S(1)} async-done(((bf16[8,2,64,576]{3,2,1,0:T(8,128)(2,1)}), bf16[8,2,64,576]{3,2,1,0:T(8,128)(2,1)S(1)}, u32[]{:S(2)}, u32[]{:S(2)}) %all-to-all-start) | async-done | bytes 1179680 | tf_op jit(solution)/shard_map/all_to_all | solution.py:45
  49.1 1.8 %gather_fusion.2 = bf16[16,64,576]{2,1,0:T(8,128)(2,1)} fusion(bf16[16,64,576]{2,1,0:T(8,128)(2,1)S(1)} %bitcast.69, s32[1024]{0:T(1024)S(1)} %pad_clamp_fusion.1), kind=kCustom, calls=%fused_computation.1.clone | custom fusion | bytes 2359360 | tf_op jit(solution)/shard_map/jit(_take)/gather | solution.py:53
  50.9 2.7 %broadcast_select_fusion = bf16[16,64,576]{2,1,0:T(8,128)(2,1)} fusion(bf16[16,64,576]{2,1,0:T(8,128)(2,1)} %gather_fusion.2, pred[16]{0:T(512)(128)(4,1)S(1)} %compare_and_fusion.1), kind=kLoop, calls=%fused_computation.17 | loop fusion | flops 589824 | bytes 2359312 | tf_op jit(solution)/shard_map/jit(_take)/select_n | solution.py:53
  53.7 0.6 gather_fusion
  54.5 0.4 fusion.38
  55.0 0.5 fusion.37
  55.4 8.8 %all-gather.2.cloned.1.call-done = bf16[2,8,2,64,576]{4,3,1,0,2:T(8,128)(2,1)} async-done(((bf16[2,8,1,64,576]{4,3,1,0,2:T(8,128)(2,1)}), bf16[2,8,2,64,576]{4,3,1,0,2:T(8,128)(2,1)}) %all-gather.2.cloned.1.call-update) | async-done | bytes 2359312 | tf_op jit(solution)/shard_map/all_gather | solution.py:54
  64.2 2.0 %copy.39 = bf16[2,8,2,64,576]{4,3,2,1,0:T(8,128)(2,1)S(1)} copy(bf16[2,8,2,64,576]{4,3,1,0,2:T(8,128)(2,1)} %all-gather.2.cloned.1.call-done) | data formatting | bytes 4718592 | tf_op jit(solution)/shard_map/all_gather | solution.py:54
  66.2 1.1 %bitcast_reduce_fusion = (f32[2,4,64]{2,1,0:T(4,128)S(1)}, f32[2,1024,4,64]{1,3,2,0:T(8,128)S(1)}) fusion(pred[2,1024]{1,0:T(4,128)(4,1)S(1)} %iota_compare_fusion, bf16[2,1024,576,1]{2,1,3,0:T(8,128)(2,1)S(1)} %bitcast.72, bf16[4,2,64,576]{3,2,1,0:T(8,128)(2,1)S(1)} %copy-done.4), kind=kOutput, calls=%fused_computation.6 | convolution fusion | flops 605552128 | bytes 5050368 | tf_op jit(solution)/shard_map/srhc,rkc->rshk/dot_general | solution.py:75
  67.4 0.3 fusion.21
  67.6 0.6 fusion.2
  68.3 0.4 convolution_bitcast_fusion.1
  68.6 1.0 %fusion.4 = f32[4,2,64,512]{3,2,0,1:T(8,128)S(1)} fusion(f32[4,2,64,512]{3,2,0,1:T(8,128)S(1)} %convolution_bitcast_fusion.1, bf16[2,1024,576]{2,1,0:T(8,128)(2,1)S(1)} %bitcast.73, f32[2,1024,4,64]{1,3,2,0:T(8,128)S(1)} %get-tuple-element.12, f32[2,4,64]{2,1,0:T(4,128)S(1)} %bitcast.81, f32[2,4,64]{2,1,0:T(4,128)S(1)} %bitcast.78, ...), kind=kOutput, calls=%fused_computation.12 | convolution fusion | flops 539754496 | bytes 6303744 | tf_op jit(solution)/shard_map/rshk,rkc->srhc/dot_general | solution.py:106
  69.7 0.4 fusion.6
  70.0 0.8 %copy.47 = bf16[4,2,64,512]{3,2,1,0:T(8,128)(2,1)} copy(bf16[4,2,64,512]{3,2,0,1:T(8,128)(2,1)S(1)} %fusion.6) | data formatting | bytes 1048576 | tf_op jit(solution)/shard_map/convert_element_type | solution.py:109
  (43 shorter events, 1.0 us)
Async XLA Ops:
  6.5 1.7 %copy-start = (bf16[1,16,64,576]{3,2,1,0:T(8,128)(2,1)S(1)}, bf16[1,16,64,576]{3,2,1,0:T(8,128)(2,1)}, u32[]{:S(2)}) copy-start(bf16[1,16,64,576]{3,2,1,0:T(8,128)(2,1)} %param.9) | copy-start | bytes 3538948
  9.0 8.7 %copy-start.3 = (s32[16]{0:T(128)S(1)}, s32[16]{0:T(128)}, u32[]{:S(2)}) copy-start(s32[16]{0:T(128)} %param.14) | copy-start | bytes 196
  10.4 38.7 %all-to-all-start = ((bf16[8,2,64,576]{3,2,1,0:T(8,128)(2,1)}), bf16[8,2,64,576]{3,2,1,0:T(8,128)(2,1)S(1)}, u32[]{:S(2)}, u32[]{:S(2)}) async-start(bf16[8,2,64,576]{3,2,1,0:T(8,128)(2,1)} %bitcast.70), calls=%async_computation | async-start | bytes 2621440 | tf_op jit(solution)/shard_map/all_to_all | solution.py:45
  17.7 46.5 %all-gather.2.cloned.1.call-start = ((), (), s32[]{:S(2)}) async-start(), calls=%async_computation.1 | async-start | bytes 3932160 | tf_op jit(solution)/shard_map/all_gather | solution.py:54
  50.9 2.8 %copy-start.2 = (bf16[4,2,576]{2,1,0:T(2,128)(2,1)S(1)}, bf16[4,2,576]{2,1,0:T(2,128)(2,1)}, u32[]{:S(2)}) copy-start(bf16[4,2,576]{2,1,0:T(2,128)(2,1)} %param.12) | copy-start | bytes 27652
  50.9 2.8 %copy-start.1 = (s32[16]{0:T(128)S(1)}, s32[16]{0:T(128)}, u32[]{:S(2)}) copy-start(s32[16]{0:T(128)} %param.13) | copy-start | bytes 196
  50.9 3.5 %copy-start.6 = (s32[2]{0:T(128)S(1)}, s32[2]{0:T(128)}, u32[]{:S(2)}) copy-start(s32[2]{0:T(128)} %param.15) | copy-start | bytes 28
  50.9 3.6 %copy-start.4 = (bf16[4,2,64,576]{3,2,1,0:T(8,128)(2,1)S(1)}, bf16[4,2,64,576]{3,2,1,0:T(8,128)(2,1)}, u32[]{:S(2)}) copy-start(bf16[4,2,64,576]{3,2,1,0:T(8,128)(2,1)} %param.11) | copy-start | bytes 1769476
  50.9 4.0 %copy-start.5 = (bf16[2,256,576]{1,2,0:T(8,128)(2,1)S(1)}, bf16[2,256,576]{1,2,0:T(8,128)(2,1)}, u32[]{:S(2)}) copy-start(bf16[2,256,576]{1,2,0:T(8,128)(2,1)} %param.10) | copy-start | bytes 1769476
Sparse Core Ops, SparseCore 0:
  53.8 10.4 all-gather.1
where the time goes:
time: 77.9 us; the launch traced here: 77.7 us
  waiting for transfers between devices  39.7 us (51%)
  between operations  13.6 us (17%)
  local copies, waits for them, and re-layouts  7.62 us (10%)
  starting transfers between devices  7.35 us (9%)
  other arithmetic  5.72 us (7%)
  matrix products  3.78 us (5%)
    all_to_all x1, waiting for transfers between devices, shards(): lax.all_to_all(rows_taken.reshape((row_count, most_slots) + local.shape[1...  30.9 us
    all_gather x1, waiting for transfers between devices, shards(): paired = lax.all_gather(mine, 'tp', axis=2, tiled=True)  8.78 us
    all_to_all x1, starting transfers between devices, shards(): lax.all_to_all(rows_taken.reshape((row_count, most_slots) + local.shape[1...  7.31 us
    select_n x2, other arithmetic, shards(): jnp.take(flat, fetch_index, axis=0)  2.71 us
    all_gather x1, local copies, waits for them, and re-layouts, shards(): paired = lax.all_gather(mine, 'tp', axis=2, tiled=True)  2 us
    gather x1, local copies, waits for them, and re-layouts, shards(): jnp.take(flat, fetch_index, axis=0)  1.79 us
  transfers between devices with their start and end apart: 2, of which 2 were waited for; matrix products, arithmetic and copies ran while one was open for 3% of the time, Pallas kernels for 0%

commit v1 on v0

v1 whole, which is shorter than its diff:
```python
import functools

import jax
import jax.numpy as jnp
from jax import lax
from jax.experimental import pallas as pl
from jax.experimental.pallas import tpu as pltpu
from jax.sharding import PartitionSpec as P


KV_RANK = 512
ROPE_DIM = 64
NOPE_DIM = 128
SPR = 8


PACK_VMEM = 4 << 20
ATTEND_VMEM = 16 << 20

SEND_ORDER = (7, 6, 5, 4, 3, 2, 1)
STAGES = ((0,), (1, 2, 3), (7, 6), (5, 4))


def pack_kernel(order, assign_ref, place_ref, latent_ref, *refs):
    outs, sems = refs[:-1], refs[-1]
    rows_here = outs[0].shape[0]
    place = place_ref[0]
    copies = []
    for i, offset in enumerate(order):
        for slot in range(rows_here):
            prompt = assign_ref[(place ^ offset) * rows_here + slot]
            copy = pltpu.make_async_copy(
                latent_ref.at[prompt], outs[i].at[slot], sems.at[i, slot]
            )
            copy.start()
            copies.append(copy)
    for copy in copies:
        copy.wait()


def pack(order, assign, place, local, rows_here):
    shape = (rows_here,) + local.shape[1:]
    return pl.pallas_call(
        functools.partial(pack_kernel, order),
        out_shape=[jax.ShapeDtypeStruct(shape, local.dtype) for _ in order],
        in_specs=[
            pl.BlockSpec(memory_space=pltpu.SMEM),
            pl.BlockSpec(memory_space=pltpu.SMEM),
            pl.BlockSpec(memory_space=pl.ANY),
        ],
        out_specs=[pl.BlockSpec(memory_space=pltpu.VMEM) for _ in order],
        scratch_shapes=[pltpu.SemaphoreType.DMA((len(order), rows_here))],
        compiler_params=pltpu.CompilerParams(vmem_limit_bytes=PACK_VMEM),
        name="pack",
    )(assign, place.reshape(1), local)


def attend_kernel(offsets, first, last, info_ref, q_ref, *refs):
    refs = list(refs)
    own = [refs.pop(0) for _ in offsets]
    other = [refs.pop(0) for _ in offsets]
    if first:
        cache_ref, new_ref = refs.pop(0), refs.pop(0)
    else:
        top_in, sum_in, acc_in = refs.pop(0), refs.pop(0), refs.pop(0)
    if last:
        out_ref = refs.pop(0)
    else:
        top_out, sum_out, acc_out = refs.pop(0), refs.pop(0), refs.pop(0)
    keys_ref = refs.pop(0)
    steps, rows, heads, width = q_ref.shape
    piece = own[0].shape[1]
    block = 2 * piece
    scale = (NOPE_DIM + ROPE_DIM) ** -0.5
    place, side = info_ref[2 * rows], info_ref[2 * rows + 1]
    for r in range(rows):
        used = 0
        masks = []
        live = info_ref[r]
        for i, offset in enumerate(offsets):
            keys_ref[r, used : used + piece] = own[i][r]
            keys_ref[r, used + piece : used + block] = other[i][r]
            lane = lax.broadcasted_iota(jnp.int32, (1, block), 1)
            flip = jnp.where(lane < piece, side, 1 - side) * piece + lane % piece
            masks.append((place ^ offset) * block + flip < live)
            used += block
        if first:
            cached = cache_ref.shape[1]
            keys_ref[r, used : used + cached] = cache_ref[r]
            lane = lax.broadcasted_iota(jnp.int32, (1, cached), 1)
            masks.append(lane < info_ref[rows + r])
            used += cached
        key = keys_ref[r, :used]
        query = q_ref[:, r].reshape(steps * heads, width)
        contract = (((1,), (1,)), ((), ()))
        scores = lax.dot_general(query, key, contract, preferred_element_type=jnp.float32)
        scores = jnp.where(jnp.concatenate(masks, axis=1), scores * scale, -jnp.inf)
        top = jnp.max(scores, axis=1, keepdims=True)
        if first:
            fresh_key = new_ref[r]
            fresh = lax.dot_general(query, fresh_key, contract, preferred_element_type=jnp.float32)
            step = lax.broadcasted_iota(jnp.int32, fresh.shape, 0) // heads
            slot = lax.broadcasted_iota(jnp.int32, fresh.shape, 1)
            fresh = jnp.where(slot <= step, fresh * scale, -jnp.inf)
            top = jnp.maximum(top, jnp.max(fresh, axis=1, keepdims=True))
        else:
            top = jnp.maximum(top, top_in[r])
        weight = jnp.exp(scores - top)
        total = jnp.sum(weight, axis=1, keepdims=True)
        acc = jnp.dot(
            weight.astype(key.dtype), key[:, :KV_RANK], preferred_element_type=jnp.float32
        )
        if first:
            fresh_weight = jnp.exp(fresh - top)
            total += jnp.sum(fresh_weight, axis=1, keepdims=True)
            acc += jnp.dot(
                fresh_weight.astype(key.dtype),
                fresh_key[:, :KV_RANK],
                preferred_element_type=jnp.float32,
            )
        else:
            shrink = jnp.exp(top_in[r] - top)
            total += shrink * sum_in[r]
            acc += shrink * acc_in[r]
        if last:
            out = (acc / total).astype(out_ref.dtype)
            out_ref[:, r] = out.reshape(steps, heads, KV_RANK)
        else:
            top_out[r] = top
            sum_out[r] = total
            acc_out[r] = acc


def attend(offsets, info, queries, own, other, cache=None, fresh=None, carry=None, last=False):
    steps, rows, heads, width = queries.shape
    first = carry is None
    keys = 2 * own[0].shape[1] * len(offsets) + (cache.shape[1] if first else 0)
    tall = steps * heads
    state = (
        jax.ShapeDtypeStruct((rows, tall, 1), jnp.float32),
        jax.ShapeDtypeStruct((rows, tall, 1), jnp.float32),
        jax.ShapeDtypeStruct((rows, tall, KV_RANK), jnp.float32),
    )
    out_shape = jax.ShapeDtypeStruct((steps, rows, heads, KV_RANK), queries.dtype) if last else state
    extra = (cache, fresh) if first else carry
    operands = (info, queries, *own, *other, *extra)
    vmem = pl.BlockSpec(memory_space=pltpu.VMEM)
    return pl.pallas_call(
        functools.partial(attend_kernel, offsets, first, last),
        out_shape=out_shape,
        in_specs=[pl.BlockSpec(memory_space=pltpu.SMEM)] + [vmem] * (len(operands) - 1),
        out_specs=vmem if last else (vmem,) * 3,
        scratch_shapes=[pltpu.VMEM((rows, keys, width), queries.dtype)],
        cost_estimate=pl.CostEstimate(
            flops=2 * rows * tall * keys * (width + KV_RANK),
            bytes_accessed=2 * rows * (keys + tall) * width,
            transcendentals=rows * tall * keys,
        ),
        compiler_params=pltpu.CompilerParams(vmem_limit_bytes=ATTEND_VMEM),
        name="attend_last" if last else "attend",
    )(*operands)


def spread_exchange(local, assign, row_place, row_count, rows_here):
    group_rows = local.shape[0]
    most_slots = min(rows_here, max(2, 2 * rows_here * SPR // row_count))
    home_group = row_place // SPR
    dest_prompt = assign.reshape(row_count, rows_here)
    in_group = dest_prompt // group_rows == home_group
    rank = jnp.cumsum(in_group.astype(jnp.int32), axis=1) - 1
    slot_ids = jnp.arange(most_slots, dtype=jnp.int32)
    picked = in_group[:, :, None] & (rank[:, :, None] == slot_ids[None, None, :])
    local_id = dest_prompt - home_group * group_rows
    source_index = jnp.sum(jnp.where(picked, local_id[:, :, None], 0), axis=1)
    rows_taken = jnp.take(local, source_index.reshape(-1), axis=0)
    moved = lax.all_to_all(
        rows_taken.reshape((row_count, most_slots) + local.shape[1:]),
        "row",
        split_axis=0,
        concat_axis=0,
        tiled=True,
    )
    owned = lax.dynamic_slice_in_dim(assign, row_place * rows_here, rows_here)
    owned_group = owned // group_rows
    row_ids = jnp.arange(rows_here, dtype=jnp.int32)
    same_before = (owned_group[:, None] == owned_group[None, :]) & (
        row_ids[None, :] < row_ids[:, None]
    )
    own_rank = jnp.sum(same_before.astype(jnp.int32), axis=1)
    flat = moved.reshape((row_count * most_slots,) + local.shape[1:])
    place = row_place % SPR
    chunks = []
    for offset in range(SPR):
        index = (owned_group * SPR + (place ^ offset)) * most_slots + own_rank
        chunks.append(jnp.take(flat, index, axis=0))
    return chunks


def shards(prompt_latent, row_cache, queries, new_latent, prompt_len, assign, row_ctx):
    row_count = lax.axis_size("row")
    row_place = lax.axis_index("row")
    side = lax.axis_index("tp")
    rows_here = row_cache.shape[0]
    local = prompt_latent[0]
    place = row_place % SPR
    swap = [(0, 1), (1, 0)]
    if row_count == SPR:
        packed = dict(zip(SEND_ORDER, pack(SEND_ORDER, assign, row_place, local, rows_here)))
        mine = {}
        for offset in SEND_ORDER:
            pairs = [(i, i ^ offset) for i in range(row_count)]
            mine[offset] = lax.ppermute(packed[offset], "row", pairs)
        mine[0] = pack((0,), assign, row_place, local, rows_here)[0]
    else:
        mine = dict(enumerate(spread_exchange(local, assign, row_place, row_count, rows_here)))
    theirs = {}
    for stage in STAGES:
        for offset in stage:
            theirs[offset] = lax.ppermute(mine[offset], "tp", swap)
    owned = lax.dynamic_slice_in_dim(assign, row_place * rows_here, rows_here)
    live_len = jnp.take(prompt_len, owned)
    info = jnp.concatenate([live_len, row_ctx, place[None], side[None]]).astype(jnp.int32)
    fresh = jnp.swapaxes(new_latent, 0, 1)
    carry = None
    for number, stage in enumerate(STAGES):
        carry = attend(
            stage,
            info,
            queries,
            [mine[offset] for offset in stage],
            [theirs[offset] for offset in stage],
            row_cache,
            fresh,
            carry,
            number == len(STAGES) - 1,
        )
    return carry


def solution(mesh):
    return jax.shard_map(
        shards,
        mesh=mesh,
        in_specs=(
            P(("group", "row"), None, "tp", None),
            P(("group", "row"), None, None),
            P(None, ("group", "row"), "tp", None),
            P(None, ("group", "row"), None),
            P("group"),
            P("group"),
            P(("group", "row")),
        ),
        out_specs=P(None, ("group", "row"), "tp", None),
        check_vma=False,
    )
```

time: 77.9 us -> 56.1 us (0.72)
  waiting for transfers between devices: 39.7 us -> 24.4 us
  between operations: 13.6 us -> 0.18 us
  Pallas kernels: 0 us -> 12.6 us
  starting transfers between devices: 7.35 us -> 13.2 us
  other arithmetic: 5.72 us -> 0.24 us
  matrix products: 3.78 us -> 0 us
  local copies, waits for them, and re-layouts: 7.62 us -> 5.35 us
    all_to_all x1 -> x0, waiting for transfers between devices: 30.9 us -> none  [shards(): lax.all_to_all(rows_taken.reshape((row_count, most_slots) + local.shape[1...]
    ppermute x0 -> x15, waiting for transfers between devices: none -> 24.4 us  [the longest x7 24.3 us: shards(): mine[offset] = lax.ppermute(packed[offset], 'row', pairs)]
    ppermute x0 -> x15, starting transfers between devices: none -> 13.2 us  [the longest x7 12.1 us: shards(): mine[offset] = lax.ppermute(packed[offset], 'row', pairs)]
    pallas_call x0 -> x6, Pallas kernels: none -> 12.6 us  [the longest x4 9.56 us: attend(): pl.pallas_call(functools.partial(attend_kernel, offsets, first, last), ou...]
    all_gather x1 -> x0, waiting for transfers between devices: 8.78 us -> none  [shards(): paired = lax.all_gather(mine, 'tp', axis=2, tiled=True)]
    all_to_all x1 -> x0, starting transfers between devices: 7.31 us -> none  [shards(): lax.all_to_all(rows_taken.reshape((row_count, most_slots) + local.shape[1...]
    unnamed x14 -> x24, local copies, waits for them, and re-layouts: 0.03 us -> 4.71 us
    select_n x4 -> x0, other arithmetic: 4.08 us -> none  [the longest x2 2.71 us: shards(): jnp.take(flat, fetch_index, axis=0)]
  transfers between devices with their start and end apart: 2 -> 15, of which waited for: 2 -> 5; matrix products, arithmetic and copies ran while one was open for 3% -> 4% of each run, Pallas kernels for 0% -> 16%
where the time goes in v1:
time: 56.1 us; the launch traced here: 55.9 us
  waiting for transfers between devices  24.4 us (43%)
  starting transfers between devices  13.2 us (24%)
  Pallas kernels  12.6 us (22%)
  local copies, waits for them, and re-layouts  5.35 us (10%)
    ppermute x7, waiting for transfers between devices, shards(): mine[offset] = lax.ppermute(packed[offset], 'row', pairs)  24.3 us
    ppermute x7, starting transfers between devices, shards(): mine[offset] = lax.ppermute(packed[offset], 'row', pairs)  12.1 us
    pallas_call x4, Pallas kernels, attend(): pl.pallas_call(functools.partial(attend_kernel, offsets, first, last), ou...  9.56 us
    unnamed x24, local copies, waits for them, and re-layouts  4.71 us
    pallas_call x2, Pallas kernels, pack(): pl.pallas_call(functools.partial(pack_kernel, order), out_shape=[jax.Shap...  3.01 us
  transfers between devices with their start and end apart: 15, of which 5 were waited for; matrix products, arithmetic and copies ran while one was open for 4% of the time, Pallas kernels for 16%

profile of v1, /device:TPU:0, one launch (start us, length us, event | category | flops | bytes accessed | tf_op | source)
XLA Modules:
  0.0 55.9 jit_solution(17796213933882203302)
XLA Ops:
  0.0 1.3 %copy-done.2 = bf16[1,16,64,576]{3,2,1,0:T(8,128)(2,1)S(1)} copy-done((bf16[1,16,64,576]{3,2,1,0:T(8,128)(2,1)S(1)}, bf16[1,16,64,576]{3,2,1,0:T(8,128)(2,1)}, u32[]{:S(2)}) %copy-start.2) | copy-done | bytes 1179672
  1.3 0.7 %copy-done.7 = s32[16]{0:T(128)S(1)} copy-done((s32[16]{0:T(128)S(1)}, s32[16]{0:T(128)}, u32[]{:S(2)}) %copy-start.7) | copy-done | bytes 88
  2.0 0.8 %pack.3.refs_0_ = bf16[2,64,576]{2,1,0:T(8,128)(2,1)S(1)} custom-call(s32[16]{0:T(128)S(1)} %copy-done.7, s32[1]{0:T(128)} %bitcast.2.place_ref, bf16[16,64,576]{2,1,0:T(8,128)(2,1)S(1)} %bitcast.7), custom_call_target="tpu_custom_call" | custom-call | tf_op jit(solution)/shard_map/pack/pallas_call | solution.py:43
  2.8 0.6 collective-permute-start.14
  3.4 2.2 %pack.2 = (bf16[2,64,576]{2,1,0:T(8,128)(2,1)S(1)}, bf16[2,64,576]{2,1,0:T(8,128)(2,1)S(1)}, bf16[2,64,576]{2,1,0:T(8,128)(2,1)S(1)}, bf16[2,64,576]{2,1,0:T(8,1...) custom-call(s32[16]{0:T(128)S(1)} %copy-done.7, ...), custom_call_target="tpu_custom_call" | custom-call | tf_op jit(solution)/shard_map/pack/pallas_call | solution.py:43
  5.6 2.6 %collective-permute-start.8 = (bf16[2,64,576]{2,1,0:T(8,128)(2,1)S(1)}, bf16[2,64,576]{2,1,0:T(8,128)(2,1)S(1)}, u32[]{:S(2)}, u32[]{:S(2)}) collective-permute-start(bf16[2,64,576]{2,1,0:T(8,128)(2,1)S(1)} %get-tuple-element.25), channel_id=1, source_target_pairs={{0,2},{2,0},{4,6},{6,4},{8,10},{10,8},{12,14},{14,12},{1,3},{3,1},... | collective-permute-start | bytes 442376 | tf_op jit(solution)/shard_map/ppermute | solution.py:212
  8.2 1.6 %collective-permute-start.9 = (bf16[2,64,576]{2,1,0:T(8,128)(2,1)S(1)}, bf16[2,64,576]{2,1,0:T(8,128)(2,1)S(1)}, u32[]{:S(2)}, u32[]{:S(2)}) collective-permute-start(bf16[2,64,576]{2,1,0:T(8,128)(2,1)S(1)} %get-tuple-element.26), channel_id=1, source_target_pairs={{0,4},{2,6},{4,0},{6,2},{8,12},{10,14},{12,8},{14,10},{1,5},{3,7},... | collective-permute-start | bytes 442376 | tf_op jit(solution)/shard_map/ppermute | solution.py:212
  9.8 4.9 %collective-permute-start.4 = (bf16[2,64,576]{2,1,0:T(8,128)(2,1)S(1)}, bf16[2,64,576]{2,1,0:T(8,128)(2,1)S(1)}, u32[]{:S(2)}, u32[]{:S(2)}) collective-permute-start(bf16[2,64,576]{2,1,0:T(8,128)(2,1)S(1)} %get-tuple-element.23), channel_id=1, source_target_pairs={{0,14},{2,12},{4,10},{6,8},{8,6},{10,4},{12,2},{14,0},{1,15},{3,13... | collective-permute-start | bytes 442376 | tf_op jit(solution)/shard_map/ppermute | solution.py:212
  14.8 0.6 %gather_fusion = s32[2]{0:T(128)S(1)} fusion(s32[16]{0:T(128)S(1)} %copy-done, s32[1024]{0:T(1024)S(1)} %pad_clamp_fusion), kind=kCustom, calls=%fused_computation | custom fusion | bytes 24 | tf_op jit(solution)/shard_map/jit(_take)/gather | solution.py:221
  15.7 1.1 %collective-permute-start = (bf16[2,64,576]{2,1,0:T(8,128)(2,1)S(1)}, bf16[2,64,576]{2,1,0:T(8,128)(2,1)S(1)}, u32[]{:S(2)}, u32[]{:S(2)}) collective-permute-start(bf16[2,64,576]{2,1,0:T(8,128)(2,1)S(1)} %get-tuple-element.21), channel_id=1, source_target_pairs={{0,10},{2,8},{4,14},{6,12},{8,2},{10,0},{12,6},{14,4},{1,11},{3,9}... | collective-permute-start | bytes 442376 | tf_op jit(solution)/shard_map/ppermute | solution.py:212
  16.8 1.6 %collective-permute-start.1 = (bf16[2,64,576]{2,1,0:T(8,128)(2,1)S(1)}, bf16[2,64,576]{2,1,0:T(8,128)(2,1)S(1)}, u32[]{:S(2)}, u32[]{:S(2)}) collective-permute-start(bf16[2,64,576]{2,1,0:T(8,128)(2,1)S(1)} %get-tuple-element.22), channel_id=1, source_target_pairs={{0,8},{2,10},{4,12},{6,14},{8,0},{10,2},{12,4},{14,6},{1,9},{3,11}... | collective-permute-start | bytes 442376 | tf_op jit(solution)/shard_map/ppermute | solution.py:212
  18.4 0.9 %collective-permute-done.10.refs_2_ = bf16[2,64,576]{2,1,0:T(8,128)(2,1)S(1)} collective-permute-done((bf16[2,64,576]{2,1,0:T(8,128)(2,1)S(1)}, bf16[2,64,576]{2,1,0:T(8,128)(2,1)S(1)}, u32[]{:S(2)}, u32[]{:S(2)}) %collective-permute-start.10) | collective-permute-done | bytes 147488 | tf_op jit(solution)/shard_map/ppermute | solution.py:212
  19.4 6.5 %collective-permute-done.4.refs_0_ = bf16[2,64,576]{2,1,0:T(8,128)(2,1)S(1)} collective-permute-done((bf16[2,64,576]{2,1,0:T(8,128)(2,1)S(1)}, bf16[2,64,576]{2,1,0:T(8,128)(2,1)S(1)}, u32[]{:S(2)}, u32[]{:S(2)}) %collective-permute-start.4) | collective-permute-done | bytes 147488 | tf_op jit(solution)/shard_map/ppermute | solution.py:212
  25.9 3.5 %collective-permute-done.5.refs_1_ = bf16[2,64,576]{2,1,0:T(8,128)(2,1)S(1)} collective-permute-done((bf16[2,64,576]{2,1,0:T(8,128)(2,1)S(1)}, bf16[2,64,576]{2,1,0:T(8,128)(2,1)S(1)}, u32[]{:S(2)}, u32[]{:S(2)}) %collective-permute-start.5) | collective-permute-done | bytes 147488 | tf_op jit(solution)/shard_map/ppermute | solution.py:212
  29.4 11.2 %collective-permute-done.refs_0_ = bf16[2,64,576]{2,1,0:T(8,128)(2,1)S(1)} collective-permute-done((bf16[2,64,576]{2,1,0:T(8,128)(2,1)S(1)}, bf16[2,64,576]{2,1,0:T(8,128)(2,1)S(1)}, u32[]{:S(2)}, u32[]{:S(2)}) %collective-permute-start) | collective-permute-done | bytes 147488 | tf_op jit(solution)/shard_map/ppermute | solution.py:212
  40.6 2.2 %collective-permute-done.1.refs_1_ = bf16[2,64,576]{2,1,0:T(8,128)(2,1)S(1)} collective-permute-done((bf16[2,64,576]{2,1,0:T(8,128)(2,1)S(1)}, bf16[2,64,576]{2,1,0:T(8,128)(2,1)S(1)}, u32[]{:S(2)}, u32[]{:S(2)}) %collective-permute-start.1) | collective-permute-done | bytes 147488 | tf_op jit(solution)/shard_map/ppermute | solution.py:212
  42.9 0.7 %copy-done.3 = bf16[2,64,576]{2,1,0:T(8,128)(2,1)} copy-done((bf16[2,64,576]{2,1,0:T(8,128)(2,1)}, bf16[2,64,576]{2,1,0:T(8,128)(2,1)S(1)}, u32[]{:S(2)}) %copy-start.3) | copy-done | bytes 147480
  43.5 0.5 collective-permute-start.2
  44.0 0.7 %copy-done.5 = bf16[2,64,576]{2,1,0:T(8,128)(2,1)} copy-done((bf16[2,64,576]{2,1,0:T(8,128)(2,1)}, bf16[2,64,576]{2,1,0:T(8,128)(2,1)S(1)}, u32[]{:S(2)}) %copy-start.5) | copy-done | bytes 147480
  44.8 1.4 %copy.11.refs_2_ = bf16[2,256,576]{2,1,0:T(8,128)(2,1)S(1)} copy(bf16[2,256,576]{1,2,0:T(8,128)(2,1)} %param.8) | data formatting | bytes 1179648 | tf_op args[1]
  46.2 2.4 %attend.3 = (f32[2,256,1]{2,1,0:T(8,128)S(1)}, f32[2,256,1]{2,1,0:T(8,128)S(1)}, f32[2,256,512]{2,1,0:T(8,128)S(1)}) custom-call(s32[6]{0:T(128)S(1)} %pad_add_fusion.info_ref, bf16[4,2,64,576]{3,2,1,0:T(8,128)(2,1)S(1)} %copy-done.1, bf16[2,64,576]{2,1,0:T(8,128)(2,1)S(1)} %pack.3.refs_0_, bf16[2,64,576]{2,1,0:T(8,128)(2,1)S(1)} %collective-permute-done.14.refs_1_, ...), custom_call_target="tpu_custom_call" | custom-call | flops 427819008 | bytes 1474560 | tf_op jit(solution)/shard_map/attend/pallas_call | solution.py:148
  48.7 2.4 %attend.4 = (f32[2,256,1]{2,1,0:T(8,128)S(1)}, f32[2,256,1]{2,1,0:T(8,128)S(1)}, f32[2,256,512]{2,1,0:T(8,128)S(1)}) custom-call(s32[6]{0:T(128)S(1)} %pad_add_fusion.info_ref, bf16[4,2,64,576]{3,2,1,0:T(8,128)(2,1)S(1)} %copy-done.1, bf16[2,64,576]{2,1,0:T(8,128)(2,1)S(1)} %collective-permute-done.8.refs_0_, ...), custom_call_target="tpu_custom_call" | custom-call | flops 427819008 | bytes 1474560 | tf_op jit(solution)/shard_map/attend/pallas_call | solution.py:148
  51.1 1.9 %attend.5 = (f32[2,256,1]{2,1,0:T(8,128)S(1)}, f32[2,256,1]{2,1,0:T(8,128)S(1)}, f32[2,256,512]{2,1,0:T(8,128)S(1)}) custom-call(s32[6]{0:T(128)S(1)} %pad_add_fusion.info_ref, bf16[4,2,64,576]{3,2,1,0:T(8,128)(2,1)S(1)} %copy-done.1, bf16[2,64,576]{2,1,0:T(8,128)(2,1)S(1)} %collective-permute-done.4.refs_0_, ...), custom_call_target="tpu_custom_call" | custom-call | flops 285212672 | bytes 1179648 | tf_op jit(solution)/shard_map/attend/pallas_call | solution.py:148
  53.1 2.8 %attend_last.1 = bf16[4,2,64,512]{3,2,1,0:T(8,128)(2,1)} custom-call(s32[6]{0:T(128)S(1)} %pad_add_fusion.info_ref, bf16[4,2,64,576]{3,2,1,0:T(8,128)(2,1)S(1)} %copy-done.1, bf16[2,64,576]{2,1,0:T(8,128)(2,1)S(1)} %collective-permute-done.refs_0_, bf16[2,64,576]{2,1,0:T(8,128)(2,1)S(1)} %collective-permute-done.1.refs_1_, ...), custom_call_target="tpu_custom_call" | custom-call | flops 285212672 | bytes 1179648 | tf_op jit(solution)/shard_map/attend_last/pallas_call | solution.py:148
  (41 shorter events, 0.6 us)
Async XLA Ops:
  0.0 14.8 %copy-start = (s32[16]{0:T(128)S(1)}, s32[16]{0:T(128)}, u32[]{:S(2)}) copy-start(s32[16]{0:T(128)} %param.11) | copy-start | bytes 196
  0.0 1.3 %copy-start.2 = (bf16[1,16,64,576]{3,2,1,0:T(8,128)(2,1)S(1)}, bf16[1,16,64,576]{3,2,1,0:T(8,128)(2,1)}, u32[]{:S(2)}) copy-start(bf16[1,16,64,576]{3,2,1,0:T(8,128)(2,1)} %param.7) | copy-start | bytes 3538948
  2.0 12.7 %copy-start.8 = (s32[16]{0:T(128)S(1)}, s32[16]{0:T(128)}, u32[]{:S(2)}) copy-start(s32[16]{0:T(128)} %assign_ref.3) | copy-start | bytes 196
  2.8 41.9 %copy-start.10 = (s32[2]{0:T(128)S(1)}, s32[2]{0:T(128)}, u32[]{:S(2)}) copy-start(s32[2]{0:T(128)} %param.13) | copy-start | bytes 28
  2.8 43.4 %copy-start.9 = (bf16[4,2,576]{2,1,0:T(2,128)(2,1)S(1)}, bf16[4,2,576]{2,1,0:T(2,128)(2,1)}, u32[]{:S(2)}) copy-start(bf16[4,2,576]{2,1,0:T(2,128)(2,1)} %param.10) | copy-start | bytes 27652
  2.8 43.4 %copy-start.1 = (bf16[4,2,64,576]{3,2,1,0:T(8,128)(2,1)S(1)}, bf16[4,2,64,576]{3,2,1,0:T(8,128)(2,1)}, u32[]{:S(2)}) copy-start(bf16[4,2,64,576]{3,2,1,0:T(8,128)(2,1)} %q_ref.7) | copy-start | bytes 1769476
  2.8 12.6 %collective-permute-start.14 = (bf16[2,64,576]{2,1,0:T(8,128)(2,1)S(1)}, bf16[2,64,576]{2,1,0:T(8,128)(2,1)S(1)}, u32[]{:S(2)}, u32[]{:S(2)}) collective-permute-start(bf16[2,64,576]{2,1,0:T(8,128)(2,1)S(1)} %pack.3.refs_0_), channel_id=1, source_target_pairs={{0,1},{1,0},{2,3},{3,2},{4,5},{5,4},{6,7},{7,6},{8,9},{9,8},{10,11... | collective-permute-start | bytes 442376 | tf_op jit(solution)/shard_map/ppermute | solution.py:219
  5.6 10.1 %collective-permute-start.8 = (bf16[2,64,576]{2,1,0:T(8,128)(2,1)S(1)}, bf16[2,64,576]{2,1,0:T(8,128)(2,1)S(1)}, u32[]{:S(2)}, u32[]{:S(2)}) collective-permute-start(bf16[2,64,576]{2,1,0:T(8,128)(2,1)S(1)} %get-tuple-element.25), channel_id=1, source_target_pairs={{0,2},{2,0},{4,6},{6,4},{8,10},{10,8},{12,14},{14,12},{1,3},{3,1},... | collective-permute-start | bytes 442376 | tf_op jit(solution)/shard_map/ppermute | solution.py:212
  8.2 8.6 %collective-permute-start.9 = (bf16[2,64,576]{2,1,0:T(8,128)(2,1)S(1)}, bf16[2,64,576]{2,1,0:T(8,128)(2,1)S(1)}, u32[]{:S(2)}, u32[]{:S(2)}) collective-permute-start(bf16[2,64,576]{2,1,0:T(8,128)(2,1)S(1)} %get-tuple-element.26), channel_id=1, source_target_pairs={{0,4},{2,6},{4,0},{6,2},{8,12},{10,14},{12,8},{14,10},{1,5},{3,7},... | collective-permute-start | bytes 442376 | tf_op jit(solution)/shard_map/ppermute | solution.py:212
  9.8 9.6 %collective-permute-start.10 = (bf16[2,64,576]{2,1,0:T(8,128)(2,1)S(1)}, bf16[2,64,576]{2,1,0:T(8,128)(2,1)S(1)}, u32[]{:S(2)}, u32[]{:S(2)}) collective-permute-start(bf16[2,64,576]{2,1,0:T(8,128)(2,1)S(1)} %get-tuple-element.27), channel_id=1, source_target_pairs={{0,6},{2,4},{4,2},{6,0},{8,14},{10,12},{12,10},{14,8},{1,7},{3,5},... | collective-permute-start | bytes 442376 | tf_op jit(solution)/shard_map/ppermute | solution.py:212
  9.8 16.1 %collective-permute-start.4 = (bf16[2,64,576]{2,1,0:T(8,128)(2,1)S(1)}, bf16[2,64,576]{2,1,0:T(8,128)(2,1)S(1)}, u32[]{:S(2)}, u32[]{:S(2)}) collective-permute-start(bf16[2,64,576]{2,1,0:T(8,128)(2,1)S(1)} %get-tuple-element.23), channel_id=1, source_target_pairs={{0,14},{2,12},{4,10},{6,8},{8,6},{10,4},{12,2},{14,0},{1,15},{3,13... | collective-permute-start | bytes 442376 | tf_op jit(solution)/shard_map/ppermute | solution.py:212
  15.5 14.0 %collective-permute-start.5 = (bf16[2,64,576]{2,1,0:T(8,128)(2,1)S(1)}, bf16[2,64,576]{2,1,0:T(8,128)(2,1)S(1)}, u32[]{:S(2)}, u32[]{:S(2)}) collective-permute-start(bf16[2,64,576]{2,1,0:T(8,128)(2,1)S(1)} %get-tuple-element.24), channel_id=1, source_target_pairs={{0,12},{2,14},{4,8},{6,10},{8,4},{10,6},{12,0},{14,2},{1,13},{3,15... | collective-permute-start | bytes 442376 | tf_op jit(solution)/shard_map/ppermute | solution.py:212
  15.7 24.9 %collective-permute-start = (bf16[2,64,576]{2,1,0:T(8,128)(2,1)S(1)}, bf16[2,64,576]{2,1,0:T(8,128)(2,1)S(1)}, u32[]{:S(2)}, u32[]{:S(2)}) collective-permute-start(bf16[2,64,576]{2,1,0:T(8,128)(2,1)S(1)} %get-tuple-element.21), channel_id=1, source_target_pairs={{0,10},{2,8},{4,14},{6,12},{8,2},{10,0},{12,6},{14,4},{1,11},{3,9}... | collective-permute-start | bytes 442376 | tf_op jit(solution)/shard_map/ppermute | solution.py:212
  16.8 26.0 %collective-permute-start.1 = (bf16[2,64,576]{2,1,0:T(8,128)(2,1)S(1)}, bf16[2,64,576]{2,1,0:T(8,128)(2,1)S(1)}, u32[]{:S(2)}, u32[]{:S(2)}) collective-permute-start(bf16[2,64,576]{2,1,0:T(8,128)(2,1)S(1)} %get-tuple-element.22), channel_id=1, source_target_pairs={{0,8},{2,10},{4,12},{6,14},{8,0},{10,2},{12,4},{14,6},{1,9},{3,11}... | collective-permute-start | bytes 442376 | tf_op jit(solution)/shard_map/ppermute | solution.py:212
  19.4 23.5 %collective-permute-start.11 = (bf16[2,64,576]{2,1,0:T(8,128)(2,1)S(1)}, bf16[2,64,576]{2,1,0:T(8,128)(2,1)S(1)}, u32[]{:S(2)}, u32[]{:S(2)}) collective-permute-start(bf16[2,64,576]{2,1,0:T(8,128)(2,1)S(1)} %collective-permute-done.8.refs_0_), channel_id=1, source_target_pairs={{0,1},{1,0},{2,3},{3,2},{4,5},{5,4},{6,7},{7,6},{8,9},{9,8},{10,11... | collective-permute-start | bytes 442376 | tf_op jit(solution)/shard_map/ppermute | solution.py:219
  25.8 18.2 %collective-permute-start.12 = (bf16[2,64,576]{2,1,0:T(8,128)(2,1)S(1)}, bf16[2,64,576]{2,1,0:T(8,128)(2,1)S(1)}, u32[]{:S(2)}, u32[]{:S(2)}) collective-permute-start(bf16[2,64,576]{2,1,0:T(8,128)(2,1)S(1)} %collective-permute-done.9.refs_1_), channel_id=1, source_target_pairs={{0,1},{1,0},{2,3},{3,2},{4,5},{5,4},{6,7},{7,6},{8,9},{9,8},{10,11... | collective-permute-start | bytes 442376 | tf_op jit(solution)/shard_map/ppermute | solution.py:219
  29.4 19.2 %collective-permute-start.13 = (bf16[2,64,576]{2,1,0:T(8,128)(2,1)S(1)}, bf16[2,64,576]{2,1,0:T(8,128)(2,1)}, u32[]{:S(2)}, u32[]{:S(2)}) collective-permute-start(bf16[2,64,576]{2,1,0:T(8,128)(2,1)S(1)} %collective-permute-done.10.refs_2_), channel_id=1, source_target_pairs={{0,1},{1,0},{2,3},{3,2},{4,5},{5,4},{6,7},{7,6},{8,9},{9,8},{10,11... | collective-permute-start | bytes 442376 | tf_op jit(solution)/shard_map/ppermute | solution.py:219
  40.6 10.5 %collective-permute-start.6 = (bf16[2,64,576]{2,1,0:T(8,128)(2,1)S(1)}, bf16[2,64,576]{2,1,0:T(8,128)(2,1)S(1)}, u32[]{:S(2)}, u32[]{:S(2)}) collective-permute-start(bf16[2,64,576]{2,1,0:T(8,128)(2,1)S(1)} %collective-permute-done.4.refs_0_), channel_id=1, source_target_pairs={{0,1},{1,0},{2,3},{3,2},{4,5},{5,4},{6,7},{7,6},{8,9},{9,8},{10,11... | collective-permute-start | bytes 442376 | tf_op jit(solution)/shard_map/ppermute | solution.py:219
  42.9 8.3 %collective-permute-start.7 = (bf16[2,64,576]{2,1,0:T(8,128)(2,1)S(1)}, bf16[2,64,576]{2,1,0:T(8,128)(2,1)S(1)}, u32[]{:S(2)}, u32[]{:S(2)}) collective-permute-start(bf16[2,64,576]{2,1,0:T(8,128)(2,1)S(1)} %collective-permute-done.5.refs_1_), channel_id=1, source_target_pairs={{0,1},{1,0},{2,3},{3,2},{4,5},{5,4},{6,7},{7,6},{8,9},{9,8},{10,11... | collective-permute-start | bytes 442376 | tf_op jit(solution)/shard_map/ppermute | solution.py:219
  42.9 0.7 %copy-start.3 = (bf16[2,64,576]{2,1,0:T(8,128)(2,1)}, bf16[2,64,576]{2,1,0:T(8,128)(2,1)S(1)}, u32[]{:S(2)}) copy-start(bf16[2,64,576]{2,1,0:T(8,128)(2,1)S(1)} %collective-permute-done.11.refs_3_) | copy-start | bytes 442372
  43.5 9.5 %collective-permute-start.2 = (bf16[2,64,576]{2,1,0:T(8,128)(2,1)S(1)}, bf16[2,64,576]{2,1,0:T(8,128)(2,1)S(1)}, u32[]{:S(2)}, u32[]{:S(2)}) collective-permute-start(bf16[2,64,576]{2,1,0:T(8,128)(2,1)S(1)} %collective-permute-done.refs_0_), channel_id=1, source_target_pairs={{0,1},{1,0},{2,3},{3,2},{4,5},{5,4},{6,7},{7,6},{8,9},{9,8},{10,11... | collective-permute-start | bytes 442376 | tf_op jit(solution)/shard_map/ppermute | solution.py:219
  44.7 8.4 %collective-permute-start.3 = (bf16[2,64,576]{2,1,0:T(8,128)(2,1)S(1)}, bf16[2,64,576]{2,1,0:T(8,128)(2,1)S(1)}, u32[]{:S(2)}, u32[]{:S(2)}) collective-permute-start(bf16[2,64,576]{2,1,0:T(8,128)(2,1)S(1)} %collective-permute-done.1.refs_1_), channel_id=1, source_target_pairs={{0,1},{1,0},{2,3},{3,2},{4,5},{5,4},{6,7},{7,6},{8,9},{9,8},{10,11... | collective-permute-start | bytes 442376 | tf_op jit(solution)/shard_map/ppermute | solution.py:219
  46.2 2.5 %copy-start.4 = (bf16[2,64,576]{2,1,0:T(8,128)(2,1)S(1)}, bf16[2,64,576]{2,1,0:T(8,128)(2,1)}, u32[]{:S(2)}) copy-start(bf16[2,64,576]{2,1,0:T(8,128)(2,1)} %copy-done.3) | copy-start | bytes 442372
  46.2 2.5 %copy-start.6 = (bf16[2,64,576]{2,1,0:T(8,128)(2,1)S(1)}, bf16[2,64,576]{2,1,0:T(8,128)(2,1)}, u32[]{:S(2)}) copy-start(bf16[2,64,576]{2,1,0:T(8,128)(2,1)} %copy-done.5) | copy-start | bytes 442372
  (2 other events, 1.3 us)

commit v2 on v1

v2 whole, which is shorter than its diff:
```python
import functools

import jax
import jax.numpy as jnp
from jax import lax
from jax.experimental import pallas as pl
from jax.experimental.pallas import tpu as pltpu
from jax.sharding import PartitionSpec as P


KV_RANK = 512
ROPE_DIM = 64
NOPE_DIM = 128
SPR = 8

PACK_VMEM = 4 << 20
ATTEND_VMEM = 16 << 20

SEND_ORDER = (4, 5, 2, 3, 1, 6, 7)
STAGES = ((0,), (4, 5), (1, 2, 3), (6,), (7,))


def write_bias(bias_ref, lives, caches, place, side, piece):
    block = 2 * piece
    lane = lax.broadcasted_iota(jnp.int32, (1, block), 1)
    spot = jnp.where(lane < piece, side * piece + lane, (1 - side) * piece + lane - piece)
    rows, cached = len(lives), bias_ref.shape[1] - SPR * block
    slot = lax.broadcasted_iota(jnp.int32, (1, cached), 1)
    for r in range(rows):
        for offset in range(SPR):
            live = spot + (place ^ offset) * block < lives[r]
            bias_ref[r : r + 1, offset * block : (offset + 1) * block] = jnp.where(
                live, 0.0, -jnp.inf
            )
        bias_ref[r : r + 1, SPR * block :] = jnp.where(slot < caches[r], 0.0, -jnp.inf)


def join_rows(rows):
    return jnp.concatenate(
        [row[:, :KV_RANK] for row in rows] + [row[:, KV_RANK:] for row in rows], axis=1
    )


def pack_kernel(order, assign_hbm, length_hbm, ctx_hbm, latent_hbm, *refs):
    outs, bias_ref = refs[: len(order)], refs[len(order)]
    assign_ref, length_ref, ctx_ref, latent_ref, sems, small_sems = refs[len(order) + 1 :]
    rows_here = ctx_hbm.shape[0]
    place, side = lax.axis_index("row"), lax.axis_index("tp")
    smalls = [
        pltpu.make_async_copy(src, dst, small_sems.at[i])
        for i, (src, dst) in enumerate(
            ((assign_hbm, assign_ref), (length_hbm, length_ref), (ctx_hbm, ctx_ref))
        )
    ]
    copies = [
        pltpu.make_async_copy(latent_hbm.at[p], latent_ref.at[p], sems.at[p])
        for p in range(latent_hbm.shape[0])
    ]
    for copy in smalls + copies:
        copy.start()
    for copy in smalls:
        copy.wait()
    lives = [length_ref[assign_ref[place * rows_here + r]] for r in range(rows_here)]
    caches = [ctx_ref[r] for r in range(rows_here)]
    write_bias(bias_ref, lives, caches, place, side, latent_hbm.shape[1])
    for copy in copies:
        copy.wait()
    for out, offset in zip(outs, order):
        first = (place ^ offset) * rows_here
        out[...] = join_rows([latent_ref[assign_ref[first + r]] for r in range(rows_here)])


def pack(order, assign, prompt_len, row_ctx, local, cached):
    rows_here = row_ctx.shape[0]
    piece, width = local.shape[1:]
    hbm = pl.BlockSpec(memory_space=pltpu.HBM)
    vmem = pl.BlockSpec(memory_space=pltpu.VMEM)
    operands = [
        pltpu.with_memory_space_constraint(x, pltpu.HBM)
        for x in (assign, prompt_len, row_ctx, local)
    ]
    out = pl.pallas_call(
        functools.partial(pack_kernel, order),
        out_shape=[jax.ShapeDtypeStruct((piece, rows_here * width), local.dtype) for _ in order]
        + [jax.ShapeDtypeStruct((rows_here, SPR * 2 * piece + cached), jnp.float32)],
        in_specs=[hbm] * 4,
        out_specs=[vmem] * (len(order) + 1),
        scratch_shapes=[
            pltpu.SMEM(assign.shape, jnp.int32),
            pltpu.SMEM(prompt_len.shape, jnp.int32),
            pltpu.SMEM(row_ctx.shape, jnp.int32),
            pltpu.VMEM(local.shape, local.dtype),
            pltpu.SemaphoreType.DMA((local.shape[0],)),
            pltpu.SemaphoreType.DMA((3,)),
        ],
        compiler_params=pltpu.CompilerParams(vmem_limit_bytes=PACK_VMEM),
        name="pack",
    )(*operands)
    return dict(zip(order, out)), out[-1]


def spread_kernel(q_ref, out_ref):
    steps, rows, heads, width = q_ref.shape
    rope = width - KV_RANK
    for r in range(rows):
        query = q_ref[:, r].reshape(steps * heads, width)
        out_ref[r, :, :KV_RANK] = query[:, :KV_RANK]
        blank = jnp.zeros((steps * heads, rope), query.dtype)
        tail = [query[:, KV_RANK:] if other == r else blank for other in range(rows)]
        out_ref[r, :, KV_RANK:] = jnp.concatenate(tail, axis=1)


def spread_queries(queries):
    steps, rows, heads, width = queries.shape
    wide = KV_RANK + rows * (width - KV_RANK)
    vmem = pl.BlockSpec(memory_space=pltpu.VMEM)
    return pl.pallas_call(
        spread_kernel,
        out_shape=jax.ShapeDtypeStruct((rows, steps * heads, wide), queries.dtype),
        in_specs=[vmem],
        out_specs=vmem,
        compiler_params=pltpu.CompilerParams(vmem_limit_bytes=PACK_VMEM),
        name="spread",
    )(queries)


def attend_kernel(offsets, heads, first, last, bias_ref, q_ref, *refs):
    refs = list(refs)
    own = [refs.pop(0) for _ in offsets]
    other = [refs.pop(0) for _ in offsets]
    if first:
        cache_ref, new_ref = refs.pop(0), refs.pop(0)
    else:
        top_in, sum_in, acc_in = refs.pop(0), refs.pop(0), refs.pop(0)
    if last:
        out_ref = refs.pop(0)
    else:
        top_out, sum_out, acc_out = refs.pop(0), refs.pop(0), refs.pop(0)
    keys_ref = refs.pop(0)
    rows, tall, _ = q_ref.shape
    piece = own[0].shape[0]
    block = 2 * piece
    scale = (NOPE_DIM + ROPE_DIM) ** -0.5
    by_width = (((1,), (1,)), ((), ()))
    dot = functools.partial(lax.dot_general, preferred_element_type=jnp.float32)
    for r in range(rows):
        biases = []
        for i, offset in enumerate(offsets):
            for half, start in ((own[i], i * block), (other[i], i * block + piece)):
                spot = slice(start, start + piece)
                keys_ref[r, spot, :KV_RANK] = half[:, r * KV_RANK : (r + 1) * KV_RANK]
                keys_ref[r, spot, KV_RANK:] = half[:, rows * KV_RANK :]
            biases.append(bias_ref[r : r + 1, offset * block : (offset + 1) * block])
        query = q_ref[r]
        scores = [dot(query, keys_ref[r], by_width) * scale + jnp.concatenate(biases, axis=1)]
        values = [lambda w, r=r: jnp.dot(w, keys_ref[r, :, :KV_RANK], preferred_element_type=jnp.float32)]
        if first:
            rope = new_ref.shape[2] - KV_RANK
            rotary = query[:, KV_RANK + r * rope : KV_RANK + (r + 1) * rope]
            narrow = jnp.concatenate([query[:, :KV_RANK], rotary], axis=1)
            cached = dot(narrow, cache_ref[r], (((1,), (0,)), ((), ())))
            scores.append(cached * scale + bias_ref[r : r + 1, SPR * block :])
            values.append(lambda w, r=r: dot(w, cache_ref[r, :KV_RANK], by_width))
            fresh = dot(narrow, new_ref[r], by_width)
            step = lax.broadcasted_iota(jnp.int32, fresh.shape, 0) // heads
            slot = lax.broadcasted_iota(jnp.int32, fresh.shape, 1)
            scores.append(jnp.where(slot <= step, fresh * scale, -jnp.inf))
            values.append(
                lambda w, r=r: jnp.dot(w, new_ref[r, :, :KV_RANK], preferred_element_type=jnp.float32)
            )
        tops = [jnp.max(part, axis=1, keepdims=True) for part in scores]
        if not first:
            tops.append(top_in[r])
        top = functools.reduce(jnp.maximum, tops)
        weights = [jnp.exp(part - top) for part in scores]
        total = sum(jnp.sum(weight, axis=1, keepdims=True) for weight in weights)
        acc = sum(value(weight.astype(q_ref.dtype)) for weight, value in zip(weights, values))
        if not first:
            shrink = jnp.exp(top_in[r] - top)
            total += shrink * sum_in[r]
            acc += shrink * acc_in[r]
        if last:
            out = (acc / total).astype(out_ref.dtype)
            out_ref[:, r] = out.reshape(tall // heads, heads, KV_RANK)
        else:
            top_out[r] = top
            sum_out[r] = total
            acc_out[r] = acc


def attend(offsets, bias, wide, own, other, shape, cache=None, fresh=None, carry=None, last=False):
    rows, tall, width = wide.shape
    heads = shape[2]
    first = carry is None
    keys = 2 * own[0].shape[0] * len(offsets)
    state = (
        jax.ShapeDtypeStruct((rows, tall, 1), jnp.float32),
        jax.ShapeDtypeStruct((rows, tall, 1), jnp.float32),
        jax.ShapeDtypeStruct((rows, tall, KV_RANK), jnp.float32),
    )
    out_shape = jax.ShapeDtypeStruct(shape[:3] + (KV_RANK,), wide.dtype) if last else state
    extra = (cache, fresh) if first else carry
    operands = (bias, wide, *own, *other, *extra)
    vmem = pl.BlockSpec(memory_space=pltpu.VMEM)
    return pl.pallas_call(
        functools.partial(attend_kernel, offsets, heads, first, last),
        out_shape=out_shape,
        in_specs=[vmem] * len(operands),
        out_specs=vmem if last else (vmem,) * 3,
        scratch_shapes=[pltpu.VMEM((rows, keys, width), wide.dtype)],
        cost_estimate=pl.CostEstimate(
            flops=2 * rows * tall * keys * (width + KV_RANK),
            bytes_accessed=2 * rows * (keys + tall) * width,
            transcendentals=rows * tall * keys,
        ),
        compiler_params=pltpu.CompilerParams(vmem_limit_bytes=ATTEND_VMEM),
        name="attend_last" if last else "attend",
    )(*operands)


def spread_exchange(local, assign, row_place, row_count, rows_here):
    group_rows = local.shape[0]
    most_slots = min(rows_here, max(2, 2 * rows_here * SPR // row_count))
    home_group = row_place // SPR
    dest_prompt = assign.reshape(row_count, rows_here)
    in_group = dest_prompt // group_rows == home_group
    rank = jnp.cumsum(in_group.astype(jnp.int32), axis=1) - 1
    slot_ids = jnp.arange(most_slots, dtype=jnp.int32)
    picked = in_group[:, :, None] & (rank[:, :, None] == slot_ids[None, None, :])
    local_id = dest_prompt - home_group * group_rows
    source_index = jnp.sum(jnp.where(picked, local_id[:, :, None], 0), axis=1)
    rows_taken = jnp.take(local, source_index.reshape(-1), axis=0)
    moved = lax.all_to_all(
        rows_taken.reshape((row_count, most_slots) + local.shape[1:]),
        "row",
        split_axis=0,
        concat_axis=0,
        tiled=True,
    )
    owned = lax.dynamic_slice_in_dim(assign, row_place * rows_here, rows_here)
    owned_group = owned // group_rows
    row_ids = jnp.arange(rows_here, dtype=jnp.int32)
    same_before = (owned_group[:, None] == owned_group[None, :]) & (
        row_ids[None, :] < row_ids[:, None]
    )
    own_rank = jnp.sum(same_before.astype(jnp.int32), axis=1)
    flat = moved.reshape((row_count * most_slots,) + local.shape[1:])
    place = row_place % SPR
    chunks = {}
    for offset in range(SPR):
        index = (owned_group * SPR + (place ^ offset)) * most_slots + own_rank
        taken = jnp.take(flat, index, axis=0)
        chunks[offset] = join_rows([taken[r] for r in range(rows_here)])
    return chunks


def spread_bias(assign, prompt_len, row_ctx, row_place, side, piece, cached):
    rows_here = row_ctx.shape[0]
    owned = lax.dynamic_slice_in_dim(assign, row_place * rows_here, rows_here)
    lives = jnp.take(prompt_len, owned)
    lane = jnp.arange(2 * piece, dtype=jnp.int32)
    spot = jnp.where(lane < piece, side * piece + lane, (1 - side) * piece + lane - piece)
    block = (row_place % SPR) ^ jnp.arange(SPR, dtype=jnp.int32)
    spots = (spot[None, :] + block[:, None] * 2 * piece).reshape(1, -1)
    slots = jnp.arange(cached, dtype=jnp.int32)[None, :]
    live = jnp.concatenate([spots < lives[:, None], slots < row_ctx[:, None]], axis=1)
    return jnp.where(live, 0.0, -jnp.inf).astype(jnp.float32)


def shards(prompt_latent, row_cache, queries, new_latent, prompt_len, assign, row_ctx):
    row_count = lax.axis_size("row")
    rows_here, cached = row_cache.shape[:2]
    local = prompt_latent[0]
    if row_count == SPR:
        packed, bias = pack((0,) + SEND_ORDER, assign, prompt_len, row_ctx, local, cached)
        mine = {0: packed[0]}
        for offset in SEND_ORDER:
            pairs = [(i, i ^ offset) for i in range(row_count)]
            mine[offset] = lax.ppermute(packed[offset], "row", pairs)
    else:
        row_place, side = lax.axis_index("row"), lax.axis_index("tp")
        mine = spread_exchange(local, assign, row_place, row_count, rows_here)
        bias = spread_bias(assign, prompt_len, row_ctx, row_place, side, local.shape[1], cached)
    theirs = {}
    for stage in STAGES:
        for offset in stage:
            theirs[offset] = lax.ppermute(mine[offset], "tp", [(0, 1), (1, 0)])
    fresh = jnp.swapaxes(new_latent, 0, 1)
    wide = spread_queries(queries)
    carry = None
    for number, stage in enumerate(STAGES):
        carry = attend(
            stage,
            bias,
            wide,
            [mine[offset] for offset in stage],
            [theirs[offset] for offset in stage],
            queries.shape,
            jnp.swapaxes(row_cache, 1, 2),
            fresh,
            carry,
            number == len(STAGES) - 1,
        )
    return carry


def solution(mesh):
    return jax.shard_map(
        shards,
        mesh=mesh,
        in_specs=(
            P(("group", "row"), None, "tp", None),
            P(("group", "row"), None, None),
            P(None, ("group", "row"), "tp", None),
            P(None, ("group", "row"), None),
            P("group"),
            P("group"),
            P(("group", "row")),
        ),
        out_specs=P(None, ("group", "row"), "tp", None),
        check_vma=False,
    )
```

time: 56.1 us -> 41.1 us (0.73)
  the two profiles are of different devices: /device:TPU:0 before, /device:TPU:17 now
where the time goes in v2:
time: 41.1 us; the launch traced here: 40.9 us
  starting transfers between devices  22.5 us (55%)
  Pallas kernels  9.26 us (23%)
  waiting for transfers between devices  9.07 us (22%)
    ppermute x7, starting transfers between devices, shards(): mine[offset] = lax.ppermute(packed[offset], 'row', pairs)  12.1 us
    ppermute x8, starting transfers between devices, shards(): theirs[offset] = lax.ppermute(mine[offset], 'tp', [(0, 1), (1, 0)])  10.3 us
    ppermute x7, waiting for transfers between devices, shards(): mine[offset] = lax.ppermute(packed[offset], 'row', pairs)  9.05 us
    pallas_call x5, Pallas kernels, attend(): pl.pallas_call(functools.partial(attend_kernel, offsets, heads, first, la...  7.44 us
    pallas_call x1, Pallas kernels, pack(): pl.pallas_call(functools.partial(pack_kernel, order), out_shape=[jax.Shap...  1.74 us
  transfers between devices with their start and end apart: 15, of which 4 were waited for; matrix products, arithmetic and copies ran while one was open for 0% of the time, Pallas kernels for 14%

profile of v2, /device:TPU:17, one launch (start us, length us, event | category | flops | bytes accessed | tf_op | source)
XLA Modules:
  0.0 40.9 jit_solution(1168154836281696400)
XLA Ops:
  0.0 1.7 %pack.1 = (bf16[64,1152]{1,0:T(8,128)(2,1)S(1)}, bf16[64,1152]{1,0:T(8,128)(2,1)S(1)}, bf16[64,1152]{1,0:T(8,128)(2,1)S(1)}, bf16[64,1152]{1,0:T(8,128)(2,1)S(1)...) custom-call(s32[16]{0:T(128)} %assign_hbm.1, ...), custom_call_target="tpu_custom_call" | custom-call | tf_op jit(solution)/shard_map/pack/pallas_call | solution.py:82
  1.8 0.7 %collective-permute-start.14 = (bf16[64,1152]{1,0:T(8,128)(2,1)S(1)}, bf16[64,1152]{1,0:T(8,128)(2,1)S(1)}, u32[]{:S(2)}, u32[]{:S(2)}) collective-permute-start(bf16[64,1152]{1,0:T(8,128)(2,1)S(1)} %get-tuple-element.34.refs_0_), channel_id=1, source_target_pairs={{0,1},{1,0},{2,3},{3,2},{4,5},{5,4},{6,7},{7,6},{8,9},{9,8},{10,11... | collective-permute-start | bytes 442376 | tf_op jit(solution)/shard_map/ppermute | solution.py:287
  2.5 3.3 %collective-permute-start.11 = (bf16[64,1152]{1,0:T(8,128)(2,1)S(1)}, bf16[64,1152]{1,0:T(8,128)(2,1)S(1)}, u32[]{:S(2)}, u32[]{:S(2)}) collective-permute-start(bf16[64,1152]{1,0:T(8,128)(2,1)S(1)} %get-tuple-element.33), channel_id=1, source_target_pairs={{0,10},{2,8},{4,14},{6,12},{8,2},{10,0},{12,6},{14,4},{1,11},{3,9}... | collective-permute-start | bytes 442376 | tf_op jit(solution)/shard_map/ppermute | solution.py:279
  5.8 0.2 collective-permute-start.4
  6.0 1.3 %collective-permute-start.5 = (bf16[64,1152]{1,0:T(8,128)(2,1)S(1)}, bf16[64,1152]{1,0:T(8,128)(2,1)S(1)}, u32[]{:S(2)}, u32[]{:S(2)}) collective-permute-start(bf16[64,1152]{1,0:T(8,128)(2,1)S(1)} %get-tuple-element.30), channel_id=1, source_target_pairs={{0,4},{2,6},{4,0},{6,2},{8,12},{10,14},{12,8},{14,10},{1,5},{3,7},... | collective-permute-start | bytes 442376 | tf_op jit(solution)/shard_map/ppermute | solution.py:279
  7.3 1.1 %collective-permute-start.6 = (bf16[64,1152]{1,0:T(8,128)(2,1)S(1)}, bf16[64,1152]{1,0:T(8,128)(2,1)S(1)}, u32[]{:S(2)}, u32[]{:S(2)}) collective-permute-start(bf16[64,1152]{1,0:T(8,128)(2,1)S(1)} %get-tuple-element.31), channel_id=1, source_target_pairs={{0,6},{2,4},{4,2},{6,0},{8,14},{10,12},{12,10},{14,8},{1,7},{3,5},... | collective-permute-start | bytes 442376 | tf_op jit(solution)/shard_map/ppermute | solution.py:279
  8.5 3.8 %collective-permute-done.10.refs_0_ = bf16[64,1152]{1,0:T(8,128)(2,1)S(1)} collective-permute-done((bf16[64,1152]{1,0:T(8,128)(2,1)S(1)}, bf16[64,1152]{1,0:T(8,128)(2,1)S(1)}, u32[]{:S(2)}, u32[]{:S(2)}) %collective-permute-start.10) | collective-permute-done | bytes 147488 | tf_op jit(solution)/shard_map/ppermute | solution.py:279
  12.2 2.6 %collective-permute-start.2 = (bf16[64,1152]{1,0:T(8,128)(2,1)S(1)}, bf16[64,1152]{1,0:T(8,128)(2,1)S(1)}, u32[]{:S(2)}, u32[]{:S(2)}) collective-permute-start(bf16[64,1152]{1,0:T(8,128)(2,1)S(1)} %get-tuple-element.28), channel_id=1, source_target_pairs={{0,12},{2,14},{4,8},{6,10},{8,4},{10,6},{12,0},{14,2},{1,13},{3,15... | collective-permute-start | bytes 442376 | tf_op jit(solution)/shard_map/ppermute | solution.py:279
  14.8 0.6 %collective-permute-done.11.refs_1_ = bf16[64,1152]{1,0:T(8,128)(2,1)S(1)} collective-permute-done((bf16[64,1152]{1,0:T(8,128)(2,1)S(1)}, bf16[64,1152]{1,0:T(8,128)(2,1)S(1)}, u32[]{:S(2)}, u32[]{:S(2)}) %collective-permute-start.11) | collective-permute-done | bytes 147488 | tf_op jit(solution)/shard_map/ppermute | solution.py:279
  15.4 3.5 %collective-permute-start = (bf16[64,1152]{1,0:T(8,128)(2,1)S(1)}, bf16[64,1152]{1,0:T(8,128)(2,1)S(1)}, u32[]{:S(2)}, u32[]{:S(2)}) collective-permute-start(bf16[64,1152]{1,0:T(8,128)(2,1)S(1)} %get-tuple-element.27), channel_id=1, source_target_pairs={{0,14},{2,12},{4,10},{6,8},{8,6},{10,4},{12,2},{14,0},{1,15},{3,13... | collective-permute-start | bytes 442376 | tf_op jit(solution)/shard_map/ppermute | solution.py:279
  19.0 0.8 %collective-permute-start.12 = (bf16[64,1152]{1,0:T(8,128)(2,1)S(1)}, bf16[64,1152]{1,0:T(8,128)(2,1)S(1)}, u32[]{:S(2)}, u32[]{:S(2)}) collective-permute-start(bf16[64,1152]{1,0:T(8,128)(2,1)S(1)} %collective-permute-done.10.refs_0_), channel_id=1, source_target_pairs={{0,1},{1,0},{2,3},{3,2},{4,5},{5,4},{6,7},{7,6},{8,9},{9,8},{10,11... | collective-permute-start | bytes 442376 | tf_op jit(solution)/shard_map/ppermute | solution.py:287
  19.7 0.1 collective-permute-start.13
  19.8 7.3 %collective-permute-start.7 = (bf16[64,1152]{1,0:T(8,128)(2,1)S(1)}, bf16[64,1152]{1,0:T(8,128)(2,1)S(1)}, u32[]{:S(2)}, u32[]{:S(2)}) collective-permute-start(bf16[64,1152]{1,0:T(8,128)(2,1)S(1)} %collective-permute-done.4.refs_0_), channel_id=1, source_target_pairs={{0,1},{1,0},{2,3},{3,2},{4,5},{5,4},{6,7},{7,6},{8,9},{9,8},{10,11... | collective-permute-start | bytes 442376 | tf_op jit(solution)/shard_map/ppermute | solution.py:287
  27.1 1.1 %collective-permute-done.2.refs_0_ = bf16[64,1152]{1,0:T(8,128)(2,1)S(1)} collective-permute-done((bf16[64,1152]{1,0:T(8,128)(2,1)S(1)}, bf16[64,1152]{1,0:T(8,128)(2,1)S(1)}, u32[]{:S(2)}, u32[]{:S(2)}) %collective-permute-start.2) | collective-permute-done | bytes 147488 | tf_op jit(solution)/shard_map/ppermute | solution.py:279
  28.2 0.5 %collective-permute-start.8 = (bf16[64,1152]{1,0:T(8,128)(2,1)S(1)}, bf16[64,1152]{1,0:T(8,128)(2,1)S(1)}, u32[]{:S(2)}, u32[]{:S(2)}) collective-permute-start(bf16[64,1152]{1,0:T(8,128)(2,1)S(1)} %collective-permute-done.5.refs_1_), channel_id=1, source_target_pairs={{0,1},{1,0},{2,3},{3,2},{4,5},{5,4},{6,7},{7,6},{8,9},{9,8},{10,11... | collective-permute-start | bytes 442376 | tf_op jit(solution)/shard_map/ppermute | solution.py:287
  28.7 3.6 %collective-permute-done.refs_0_ = bf16[64,1152]{1,0:T(8,128)(2,1)S(1)} collective-permute-done((bf16[64,1152]{1,0:T(8,128)(2,1)S(1)}, bf16[64,1152]{1,0:T(8,128)(2,1)S(1)}, u32[]{:S(2)}, u32[]{:S(2)}) %collective-permute-start) | collective-permute-done | bytes 147488 | tf_op jit(solution)/shard_map/ppermute | solution.py:279
  32.3 0.4 %collective-permute-start.9 = (bf16[64,1152]{1,0:T(8,128)(2,1)S(1)}, bf16[64,1152]{1,0:T(8,128)(2,1)S(1)}, u32[]{:S(2)}, u32[]{:S(2)}) collective-permute-start(bf16[64,1152]{1,0:T(8,128)(2,1)S(1)} %collective-permute-done.6.refs_2_), channel_id=1, source_target_pairs={{0,1},{1,0},{2,3},{3,2},{4,5},{5,4},{6,7},{7,6},{8,9},{9,8},{10,11... | collective-permute-start | bytes 442376 | tf_op jit(solution)/shard_map/ppermute | solution.py:287
  32.9 0.4 %collective-permute-start.1 = (bf16[64,1152]{1,0:T(8,128)(2,1)S(1)}, bf16[64,1152]{1,0:T(8,128)(2,1)S(1)}, u32[]{:S(2)}, u32[]{:S(2)}) collective-permute-start(bf16[64,1152]{1,0:T(8,128)(2,1)S(1)} %collective-permute-done.refs_0_), channel_id=1, source_target_pairs={{0,1},{1,0},{2,3},{3,2},{4,5},{5,4},{6,7},{7,6},{8,9},{9,8},{10,11... | collective-permute-start | bytes 442376 | tf_op jit(solution)/shard_map/ppermute | solution.py:287
  33.3 0.1 spread.1.q_ref
  33.4 1.6 %attend.4 = (f32[2,256,1]{2,1,0:T(8,128)S(1)}, f32[2,256,1]{2,1,0:T(8,128)S(1)}, f32[2,256,512]{2,1,0:T(8,128)S(1)}) custom-call(f32[2,1280]{1,0:T(2,128)S(1)} %get-tuple-element.26.bias_ref, bf16[2,256,640]{2,1,0:T(8,128)(2,1)S(1)} %spread.1.q_ref, bf16[64,1152]{1,0:T(8,128)(2,1)S(1)} %get-tuple-element.34.refs_0_, ...), custom_call_target="tpu_custom_call" | custom-call | flops 150994944 | bytes 983040 | tf_op jit(solution)/shard_map/attend/pallas_call | solution.py:205
  35.0 1.4 %attend.5 = (f32[2,256,1]{2,1,0:T(8,128)S(1)}, f32[2,256,1]{2,1,0:T(8,128)S(1)}, f32[2,256,512]{2,1,0:T(8,128)S(1)}) custom-call(f32[2,1280]{1,0:T(2,128)S(1)} %get-tuple-element.26.bias_ref, bf16[2,256,640]{2,1,0:T(8,128)(2,1)S(1)} %spread.1.q_ref, bf16[64,1152]{1,0:T(8,128)(2,1)S(1)} %collective-permute-done.10.refs_0_, ...), custom_call_target="tpu_custom_call" | custom-call | flops 301989888 | bytes 1310720 | tf_op jit(solution)/shard_map/attend/pallas_call | solution.py:205
  36.5 1.5 %attend.6 = (f32[2,256,1]{2,1,0:T(8,128)S(1)}, f32[2,256,1]{2,1,0:T(8,128)S(1)}, f32[2,256,512]{2,1,0:T(8,128)S(1)}) custom-call(f32[2,1280]{1,0:T(2,128)S(1)} %get-tuple-element.26.bias_ref, bf16[2,256,640]{2,1,0:T(8,128)(2,1)S(1)} %spread.1.q_ref, bf16[64,1152]{1,0:T(8,128)(2,1)S(1)} %collective-permute-done.4.refs_0_, ...), custom_call_target="tpu_custom_call" | custom-call | flops 452984832 | bytes 1638400 | tf_op jit(solution)/shard_map/attend/pallas_call | solution.py:205
  38.0 1.1 %attend.7 = (f32[2,256,1]{2,1,0:T(8,128)S(1)}, f32[2,256,1]{2,1,0:T(8,128)S(1)}, f32[2,256,512]{2,1,0:T(8,128)S(1)}) custom-call(f32[2,1280]{1,0:T(2,128)S(1)} %get-tuple-element.26.bias_ref, bf16[2,256,640]{2,1,0:T(8,128)(2,1)S(1)} %spread.1.q_ref, bf16[64,1152]{1,0:T(8,128)(2,1)S(1)} %collective-permute-done.2.refs_0_, ...), custom_call_target="tpu_custom_call" | custom-call | flops 150994944 | bytes 983040 | tf_op jit(solution)/shard_map/attend/pallas_call | solution.py:205
  39.1 1.8 %attend_last.1 = bf16[4,2,64,512]{3,2,1,0:T(8,128)(2,1)} custom-call(f32[2,1280]{1,0:T(2,128)S(1)} %get-tuple-element.26.bias_ref, bf16[2,256,640]{2,1,0:T(8,128)(2,1)S(1)} %spread.1.q_ref, bf16[64,1152]{1,0:T(8,128)(2,1)S(1)} %collective-permute-done.refs_0_, bf16[64,1152]{1,0:T(8,128)(2,1)S(1)} %collective-permute-done.1.refs_1_, ...), custom_call_target="tpu_custom_call" | custom-call | flops 150994944 | bytes 983040 | tf_op jit(solution)/shard_map/attend_last/pallas_call | solution.py:205
  (20 shorter events, 0.1 us)
Async XLA Ops:
  0.0 33.3 %copy-start = (bf16[4,2,64,576]{3,2,1,0:T(8,128)(2,1)S(1)}, bf16[4,2,64,576]{3,2,1,0:T(8,128)(2,1)}, u32[]{:S(2)}) copy-start(bf16[4,2,64,576]{3,2,1,0:T(8,128)(2,1)} %q_ref.1) | copy-start | bytes 1769476
  0.0 33.4 %copy-start.2 = (bf16[4,2,576]{2,1,0:T(2,128)(2,1)S(1)}, bf16[4,2,576]{2,1,0:T(2,128)(2,1)}, u32[]{:S(2)}) copy-start(bf16[4,2,576]{2,1,0:T(2,128)(2,1)} %param.10) | copy-start | bytes 27652
  0.0 33.4 %copy-start.1 = (bf16[2,256,576]{1,2,0:T(8,128)(2,1)S(1)}, bf16[2,256,576]{1,2,0:T(8,128)(2,1)}, u32[]{:S(2)}) copy-start(bf16[2,256,576]{1,2,0:T(8,128)(2,1)} %param.8) | copy-start | bytes 1769476
  1.8 5.6 %collective-permute-start.14 = (bf16[64,1152]{1,0:T(8,128)(2,1)S(1)}, bf16[64,1152]{1,0:T(8,128)(2,1)S(1)}, u32[]{:S(2)}, u32[]{:S(2)}) collective-permute-start(bf16[64,1152]{1,0:T(8,128)(2,1)S(1)} %get-tuple-element.34.refs_0_), channel_id=1, source_target_pairs={{0,1},{1,0},{2,3},{3,2},{4,5},{5,4},{6,7},{7,6},{8,9},{9,8},{10,11... | collective-permute-start | bytes 442376 | tf_op jit(solution)/shard_map/ppermute | solution.py:287
  2.5 9.7 %collective-permute-start.10 = (bf16[64,1152]{1,0:T(8,128)(2,1)S(1)}, bf16[64,1152]{1,0:T(8,128)(2,1)S(1)}, u32[]{:S(2)}, u32[]{:S(2)}) collective-permute-start(bf16[64,1152]{1,0:T(8,128)(2,1)S(1)} %get-tuple-element.32), channel_id=1, source_target_pairs={{0,8},{2,10},{4,12},{6,14},{8,0},{10,2},{12,4},{14,6},{1,9},{3,11}... | collective-permute-start | bytes 442376 | tf_op jit(solution)/shard_map/ppermute | solution.py:279
  2.5 12.9 %collective-permute-start.11 = (bf16[64,1152]{1,0:T(8,128)(2,1)S(1)}, bf16[64,1152]{1,0:T(8,128)(2,1)S(1)}, u32[]{:S(2)}, u32[]{:S(2)}) collective-permute-start(bf16[64,1152]{1,0:T(8,128)(2,1)S(1)} %get-tuple-element.33), channel_id=1, source_target_pairs={{0,10},{2,8},{4,14},{6,12},{8,2},{10,0},{12,6},{14,4},{1,11},{3,9}... | collective-permute-start | bytes 442376 | tf_op jit(solution)/shard_map/ppermute | solution.py:279
  5.8 13.1 %collective-permute-start.4 = (bf16[64,1152]{1,0:T(8,128)(2,1)S(1)}, bf16[64,1152]{1,0:T(8,128)(2,1)S(1)}, u32[]{:S(2)}, u32[]{:S(2)}) collective-permute-start(bf16[64,1152]{1,0:T(8,128)(2,1)S(1)} %get-tuple-element.29), channel_id=1, source_target_pairs={{0,2},{2,0},{4,6},{6,4},{8,10},{10,8},{12,14},{14,12},{1,3},{3,1},... | collective-permute-start | bytes 442376 | tf_op jit(solution)/shard_map/ppermute | solution.py:279
  6.0 13.7 %collective-permute-start.5 = (bf16[64,1152]{1,0:T(8,128)(2,1)S(1)}, bf16[64,1152]{1,0:T(8,128)(2,1)S(1)}, u32[]{:S(2)}, u32[]{:S(2)}) collective-permute-start(bf16[64,1152]{1,0:T(8,128)(2,1)S(1)} %get-tuple-element.30), channel_id=1, source_target_pairs={{0,4},{2,6},{4,0},{6,2},{8,12},{10,14},{12,8},{14,10},{1,5},{3,7},... | collective-permute-start | bytes 442376 | tf_op jit(solution)/shard_map/ppermute | solution.py:279
  7.3 12.5 %collective-permute-start.6 = (bf16[64,1152]{1,0:T(8,128)(2,1)S(1)}, bf16[64,1152]{1,0:T(8,128)(2,1)S(1)}, u32[]{:S(2)}, u32[]{:S(2)}) collective-permute-start(bf16[64,1152]{1,0:T(8,128)(2,1)S(1)} %get-tuple-element.31), channel_id=1, source_target_pairs={{0,6},{2,4},{4,2},{6,0},{8,14},{10,12},{12,10},{14,8},{1,7},{3,5},... | collective-permute-start | bytes 442376 | tf_op jit(solution)/shard_map/ppermute | solution.py:279
  12.2 16.0 %collective-permute-start.2 = (bf16[64,1152]{1,0:T(8,128)(2,1)S(1)}, bf16[64,1152]{1,0:T(8,128)(2,1)S(1)}, u32[]{:S(2)}, u32[]{:S(2)}) collective-permute-start(bf16[64,1152]{1,0:T(8,128)(2,1)S(1)} %get-tuple-element.28), channel_id=1, source_target_pairs={{0,12},{2,14},{4,8},{6,10},{8,4},{10,6},{12,0},{14,2},{1,13},{3,15... | collective-permute-start | bytes 442376 | tf_op jit(solution)/shard_map/ppermute | solution.py:279
  15.4 16.9 %collective-permute-start = (bf16[64,1152]{1,0:T(8,128)(2,1)S(1)}, bf16[64,1152]{1,0:T(8,128)(2,1)S(1)}, u32[]{:S(2)}, u32[]{:S(2)}) collective-permute-start(bf16[64,1152]{1,0:T(8,128)(2,1)S(1)} %get-tuple-element.27), channel_id=1, source_target_pairs={{0,14},{2,12},{4,10},{6,8},{8,6},{10,4},{12,2},{14,0},{1,15},{3,13... | collective-permute-start | bytes 442376 | tf_op jit(solution)/shard_map/ppermute | solution.py:279
  19.0 13.8 %collective-permute-start.12 = (bf16[64,1152]{1,0:T(8,128)(2,1)S(1)}, bf16[64,1152]{1,0:T(8,128)(2,1)S(1)}, u32[]{:S(2)}, u32[]{:S(2)}) collective-permute-start(bf16[64,1152]{1,0:T(8,128)(2,1)S(1)} %collective-permute-done.10.refs_0_), channel_id=1, source_target_pairs={{0,1},{1,0},{2,3},{3,2},{4,5},{5,4},{6,7},{7,6},{8,9},{9,8},{10,11... | collective-permute-start | bytes 442376 | tf_op jit(solution)/shard_map/ppermute | solution.py:287
  19.7 13.1 %collective-permute-start.13 = (bf16[64,1152]{1,0:T(8,128)(2,1)S(1)}, bf16[64,1152]{1,0:T(8,128)(2,1)S(1)}, u32[]{:S(2)}, u32[]{:S(2)}) collective-permute-start(bf16[64,1152]{1,0:T(8,128)(2,1)S(1)} %collective-permute-done.11.refs_1_), channel_id=1, source_target_pairs={{0,1},{1,0},{2,3},{3,2},{4,5},{5,4},{6,7},{7,6},{8,9},{9,8},{10,11... | collective-permute-start | bytes 442376 | tf_op jit(solution)/shard_map/ppermute | solution.py:287
  19.8 16.6 %collective-permute-start.7 = (bf16[64,1152]{1,0:T(8,128)(2,1)S(1)}, bf16[64,1152]{1,0:T(8,128)(2,1)S(1)}, u32[]{:S(2)}, u32[]{:S(2)}) collective-permute-start(bf16[64,1152]{1,0:T(8,128)(2,1)S(1)} %collective-permute-done.4.refs_0_), channel_id=1, source_target_pairs={{0,1},{1,0},{2,3},{3,2},{4,5},{5,4},{6,7},{7,6},{8,9},{9,8},{10,11... | collective-permute-start | bytes 442376 | tf_op jit(solution)/shard_map/ppermute | solution.py:287
  28.2 8.2 %collective-permute-start.8 = (bf16[64,1152]{1,0:T(8,128)(2,1)S(1)}, bf16[64,1152]{1,0:T(8,128)(2,1)S(1)}, u32[]{:S(2)}, u32[]{:S(2)}) collective-permute-start(bf16[64,1152]{1,0:T(8,128)(2,1)S(1)} %collective-permute-done.5.refs_1_), channel_id=1, source_target_pairs={{0,1},{1,0},{2,3},{3,2},{4,5},{5,4},{6,7},{7,6},{8,9},{9,8},{10,11... | collective-permute-start | bytes 442376 | tf_op jit(solution)/shard_map/ppermute | solution.py:287
  32.3 4.1 %collective-permute-start.9 = (bf16[64,1152]{1,0:T(8,128)(2,1)S(1)}, bf16[64,1152]{1,0:T(8,128)(2,1)S(1)}, u32[]{:S(2)}, u32[]{:S(2)}) collective-permute-start(bf16[64,1152]{1,0:T(8,128)(2,1)S(1)} %collective-permute-done.6.refs_2_), channel_id=1, source_target_pairs={{0,1},{1,0},{2,3},{3,2},{4,5},{5,4},{6,7},{7,6},{8,9},{9,8},{10,11... | collective-permute-start | bytes 442376 | tf_op jit(solution)/shard_map/ppermute | solution.py:287
  32.8 5.2 %collective-permute-start.3 = (bf16[64,1152]{1,0:T(8,128)(2,1)S(1)}, bf16[64,1152]{1,0:T(8,128)(2,1)S(1)}, u32[]{:S(2)}, u32[]{:S(2)}) collective-permute-start(bf16[64,1152]{1,0:T(8,128)(2,1)S(1)} %collective-permute-done.2.refs_0_), channel_id=1, source_target_pairs={{0,1},{1,0},{2,3},{3,2},{4,5},{5,4},{6,7},{7,6},{8,9},{9,8},{10,11... | collective-permute-start | bytes 442376 | tf_op jit(solution)/shard_map/ppermute | solution.py:287
  32.9 6.3 %collective-permute-start.1 = (bf16[64,1152]{1,0:T(8,128)(2,1)S(1)}, bf16[64,1152]{1,0:T(8,128)(2,1)S(1)}, u32[]{:S(2)}, u32[]{:S(2)}) collective-permute-start(bf16[64,1152]{1,0:T(8,128)(2,1)S(1)} %collective-permute-done.refs_0_), channel_id=1, source_target_pairs={{0,1},{1,0},{2,3},{3,2},{4,5},{5,4},{6,7},{7,6},{8,9},{9,8},{10,11... | collective-permute-start | bytes 442376 | tf_op jit(solution)/shard_map/ppermute | solution.py:287

commit v3 on v2

--- a/solution.py
+++ b/solution.py
@@ -17,7 +17,7 @@
 ATTEND_VMEM = 16 << 20
 
 SEND_ORDER = (4, 5, 2, 3, 1, 6, 7)
-STAGES = ((0,), (4, 5), (1, 2, 3), (6,), (7,))
+STAGES = ((0,), (4, 5), (1, 2, 3, 6), (7,))
 
 
 def write_bias(bias_ref, lives, caches, place, side, piece):
@@ -70,15 +70,14 @@
         out[...] = join_rows([latent_ref[assign_ref[first + r]] for r in range(rows_here)])
 
 
+def in_hbm(*arrays):
+    return [pltpu.with_memory_space_constraint(x, pltpu.HBM) for x in arrays]
+
+
 def pack(order, assign, prompt_len, row_ctx, local, cached):
     rows_here = row_ctx.shape[0]
-    piece, width = local.shape[1:]
-    hbm = pl.BlockSpec(memory_space=pltpu.HBM)
-    vmem = pl.BlockSpec(memory_space=pltpu.VMEM)
-    operands = [
-        pltpu.with_memory_space_constraint(x, pltpu.HBM)
-        for x in (assign, prompt_len, row_ctx, local)
-    ]
+    count, piece, width = local.shape
+    hbm, vmem = pl.BlockSpec(memory_space=pltpu.HBM), pl.BlockSpec(memory_space=pltpu.VMEM)
     out = pl.pallas_call(
         functools.partial(pack_kernel, order),
         out_shape=[jax.ShapeDtypeStruct((piece, rows_here * width), local.dtype) for _ in order]
@@ -90,16 +89,23 @@
             pltpu.SMEM(prompt_len.shape, jnp.int32),
             pltpu.SMEM(row_ctx.shape, jnp.int32),
             pltpu.VMEM(local.shape, local.dtype),
-            pltpu.SemaphoreType.DMA((local.shape[0],)),
+            pltpu.SemaphoreType.DMA((count,)),
             pltpu.SemaphoreType.DMA((3,)),
         ],
         compiler_params=pltpu.CompilerParams(vmem_limit_bytes=PACK_VMEM),
         name="pack",
-    )(*operands)
+    )(*in_hbm(assign, prompt_len, row_ctx, local))
     return dict(zip(order, out)), out[-1]
 
 
-def spread_kernel(q_ref, out_ref):
+def spread_kernel(q_hbm, cache_hbm, out_ref, cache_ref, q_ref, sems):
+    copies = [
+        pltpu.make_async_copy(q_hbm, q_ref, sems.at[0]),
+        pltpu.make_async_copy(cache_hbm, cache_ref, sems.at[1]),
+    ]
+    for copy in copies:
+        copy.start()
+    copies[0].wait()
     steps, rows, heads, width = q_ref.shape
     rope = width - KV_RANK
     for r in range(rows):
@@ -108,20 +114,28 @@
         blank = jnp.zeros((steps * heads, rope), query.dtype)
         tail = [query[:, KV_RANK:] if other == r else blank for other in range(rows)]
         out_ref[r, :, KV_RANK:] = jnp.concatenate(tail, axis=1)
-
-
-def spread_queries(queries):
+    copies[1].wait()
+
+
+def spread_queries(queries, turned):
     steps, rows, heads, width = queries.shape
     wide = KV_RANK + rows * (width - KV_RANK)
-    vmem = pl.BlockSpec(memory_space=pltpu.VMEM)
+    hbm, vmem = pl.BlockSpec(memory_space=pltpu.HBM), pl.BlockSpec(memory_space=pltpu.VMEM)
     return pl.pallas_call(
         spread_kernel,
-        out_shape=jax.ShapeDtypeStruct((rows, steps * heads, wide), queries.dtype),
-        in_specs=[vmem],
-        out_specs=vmem,
+        out_shape=[
+            jax.ShapeDtypeStruct((rows, steps * heads, wide), queries.dtype),
+            jax.ShapeDtypeStruct(turned.shape, turned.dtype),
+        ],
+        in_specs=[hbm] * 2,
+        out_specs=[vmem] * 2,
+        scratch_shapes=[
+            pltpu.VMEM(queries.shape, queries.dtype),
+            pltpu.SemaphoreType.DMA((2,)),
+        ],
         compiler_params=pltpu.CompilerParams(vmem_limit_bytes=PACK_VMEM),
         name="spread",
-    )(queries)
+    )(*in_hbm(queries, turned))
 
 
 def attend_kernel(offsets, heads, first, last, bias_ref, q_ref, *refs):
@@ -133,10 +147,9 @@
     else:
         top_in, sum_in, acc_in = refs.pop(0), refs.pop(0), refs.pop(0)
     if last:
-        out_ref = refs.pop(0)
+        out_ref, stage_ref, sems = refs
     else:
-        top_out, sum_out, acc_out = refs.pop(0), refs.pop(0), refs.pop(0)
-    keys_ref = refs.pop(0)
+        top_out, sum_out, acc_out = refs
     rows, tall, _ = q_ref.shape
     piece = own[0].shape[0]
     block = 2 * piece
@@ -144,20 +157,18 @@
     by_width = (((1,), (1,)), ((), ()))
     dot = functools.partial(lax.dot_general, preferred_element_type=jnp.float32)
     for r in range(rows):
-        biases = []
-        for i, offset in enumerate(offsets):
-            for half, start in ((own[i], i * block), (other[i], i * block + piece)):
-                spot = slice(start, start + piece)
-                keys_ref[r, spot, :KV_RANK] = half[:, r * KV_RANK : (r + 1) * KV_RANK]
-                keys_ref[r, spot, KV_RANK:] = half[:, rows * KV_RANK :]
-            biases.append(bias_ref[r : r + 1, offset * block : (offset + 1) * block])
+        halves = [half for pair in zip(own, other) for half in pair]
+        value = jnp.concatenate([h[:, r * KV_RANK : (r + 1) * KV_RANK] for h in halves], axis=0)
+        rotary = jnp.concatenate([h[:, rows * KV_RANK :] for h in halves], axis=0)
+        biases = [bias_ref[r : r + 1, i * block : (i + 1) * block] for i in offsets]
         query = q_ref[r]
-        scores = [dot(query, keys_ref[r], by_width) * scale + jnp.concatenate(biases, axis=1)]
-        values = [lambda w, r=r: jnp.dot(w, keys_ref[r, :, :KV_RANK], preferred_element_type=jnp.float32)]
+        found = dot(query, jnp.concatenate([value, rotary], axis=1), by_width)
+        scores = [found * scale + jnp.concatenate(biases, axis=1)]
+        values = [lambda w, v=value: jnp.dot(w, v, preferred_element_type=jnp.float32)]
         if first:
             rope = new_ref.shape[2] - KV_RANK
-            rotary = query[:, KV_RANK + r * rope : KV_RANK + (r + 1) * rope]
-            narrow = jnp.concatenate([query[:, :KV_RANK], rotary], axis=1)
+            turn = query[:, KV_RANK + r * rope : KV_RANK + (r + 1) * rope]
+            narrow = jnp.concatenate([query[:, :KV_RANK], turn], axis=1)
             cached = dot(narrow, cache_ref[r], (((1,), (0,)), ((), ())))
             scores.append(cached * scale + bias_ref[r : r + 1, SPR * block :])
             values.append(lambda w, r=r: dot(w, cache_ref[r, :KV_RANK], by_width))
@@ -174,23 +185,33 @@
         top = functools.reduce(jnp.maximum, tops)
         weights = [jnp.exp(part - top) for part in scores]
         total = sum(jnp.sum(weight, axis=1, keepdims=True) for weight in weights)
-        acc = sum(value(weight.astype(q_ref.dtype)) for weight, value in zip(weights, values))
+        acc = sum(times(weight.astype(q_ref.dtype)) for weight, times in zip(weights, values))
         if not first:
             shrink = jnp.exp(top_in[r] - top)
             total += shrink * sum_in[r]
             acc += shrink * acc_in[r]
         if last:
-            out = (acc / total).astype(out_ref.dtype)
-            out_ref[:, r] = out.reshape(tall // heads, heads, KV_RANK)
+            out = (acc * (1.0 / total)).astype(out_ref.dtype)
+            stage_ref[r] = out.reshape(tall // heads, heads, KV_RANK)
+            copies = [
+                pltpu.make_async_copy(stage_ref.at[r, s], out_ref.at[s, r], sems.at[r, s])
+                for s in range(tall // heads)
+            ]
+            for copy in copies:
+                copy.start()
         else:
             top_out[r] = top
             sum_out[r] = total
             acc_out[r] = acc
-
-
-def attend(offsets, bias, wide, own, other, shape, cache=None, fresh=None, carry=None, last=False):
+    if last:
+        for r in range(rows):
+            for s in range(tall // heads):
+                pltpu.make_async_copy(stage_ref.at[r, s], out_ref.at[s, r], sems.at[r, s]).wait()
+
+
+def attend(offsets, bias, wide, own, other, shape, cache, fresh, carry, last):
     rows, tall, width = wide.shape
-    heads = shape[2]
+    steps, heads = shape[0], shape[2]
     first = carry is None
     keys = 2 * own[0].shape[0] * len(offsets)
     state = (
@@ -198,16 +219,21 @@
         jax.ShapeDtypeStruct((rows, tall, 1), jnp.float32),
         jax.ShapeDtypeStruct((rows, tall, KV_RANK), jnp.float32),
     )
-    out_shape = jax.ShapeDtypeStruct(shape[:3] + (KV_RANK,), wide.dtype) if last else state
-    extra = (cache, fresh) if first else carry
-    operands = (bias, wide, *own, *other, *extra)
-    vmem = pl.BlockSpec(memory_space=pltpu.VMEM)
+    final = (steps, rows, heads, KV_RANK)
+    operands = (bias, wide, *own, *other, *((cache, fresh) if first else carry))
+    vmem, hbm = pl.BlockSpec(memory_space=pltpu.VMEM), pl.BlockSpec(memory_space=pltpu.HBM)
+    scratch = []
+    if last:
+        scratch = [
+            pltpu.VMEM((rows, steps, heads, KV_RANK), wide.dtype),
+            pltpu.SemaphoreType.DMA((rows, steps)),
+        ]
     return pl.pallas_call(
         functools.partial(attend_kernel, offsets, heads, first, last),
-        out_shape=out_shape,
+        out_shape=jax.ShapeDtypeStruct(final, wide.dtype) if last else state,
         in_specs=[vmem] * len(operands),
-        out_specs=vmem if last else (vmem,) * 3,
-        scratch_shapes=[pltpu.VMEM((rows, keys, width), wide.dtype)],
+        out_specs=hbm if last else (vmem,) * 3,
+        scratch_shapes=scratch,
         cost_estimate=pl.CostEstimate(
             flops=2 * rows * tall * keys * (width + KV_RANK),
             bytes_accessed=2 * rows * (keys + tall) * width,
@@ -272,7 +298,7 @@
     rows_here, cached = row_cache.shape[:2]
     local = prompt_latent[0]
     if row_count == SPR:
-        packed, bias = pack((0,) + SEND_ORDER, assign, prompt_len, row_ctx, local, cached)
+        packed, bias = pack(SEND_ORDER + (0,), assign, prompt_len, row_ctx, local, cached)
         mine = {0: packed[0]}
         for offset in SEND_ORDER:
             pairs = [(i, i ^ offset) for i in range(row_count)]
@@ -286,20 +312,13 @@
         for offset in stage:
             theirs[offset] = lax.ppermute(mine[offset], "tp", [(0, 1), (1, 0)])
     fresh = jnp.swapaxes(new_latent, 0, 1)
-    wide = spread_queries(queries)
+    wide, turned = spread_queries(queries, jnp.swapaxes(row_cache, 1, 2))
     carry = None
     for number, stage in enumerate(STAGES):
+        own, other = [mine[offset] for offset in stage], [theirs[offset] for offset in stage]
+        last = number == len(STAGES) - 1
         carry = attend(
-            stage,
-            bias,
-            wide,
-            [mine[offset] for offset in stage],
-            [theirs[offset] for offset in stage],
-            queries.shape,
-            jnp.swapaxes(row_cache, 1, 2),
-            fresh,
-            carry,
-            number == len(STAGES) - 1,
+            stage, bias, wide, own, other, queries.shape, turned, fresh, carry, last
         )
     return carry
 

time: 41.1 us -> 41.1 us (level)
    pallas_call x1, Pallas kernels: 0.09 us -> 1.28 us  [spread_queries(): pl.pallas_call(spread_kernel, out_shape=[jax.ShapeDtypeStruct((rows, step...]
    pallas_call x5 -> x4, Pallas kernels: 7.44 us -> 6.33 us  [attend(): pl.pallas_call(functools.partial(attend_kernel, offsets, heads, first, la...]
where the time goes in v3:
time: 41.1 us; the launch traced here: 40.9 us
  starting transfers between devices  22.5 us (55%)
  Pallas kernels  9.26 us (23%)
  waiting for transfers between devices  9.07 us (22%)
    ppermute x7, starting transfers between devices, shards(): mine[offset] = lax.ppermute(packed[offset], 'row', pairs)  12.1 us
    ppermute x8, starting transfers between devices, shards(): theirs[offset] = lax.ppermute(mine[offset], 'tp', [(0, 1), (1, 0)])  10.3 us
    ppermute x7, waiting for transfers between devices, shards(): mine[offset] = lax.ppermute(packed[offset], 'row', pairs)  9.05 us
    pallas_call x4, Pallas kernels, attend(): pl.pallas_call(functools.partial(attend_kernel, offsets, heads, first, la...  6.33 us
    pallas_call x1, Pallas kernels, pack(): pl.pallas_call(functools.partial(pack_kernel, order), out_shape=[jax.Shap...  1.65 us
    pallas_call x1, Pallas kernels, spread_queries(): pl.pallas_call(spread_kernel, out_shape=[jax.ShapeDtypeStruct((rows, step...  1.28 us
  transfers between devices with their start and end apart: 15, of which 4 were waited for; matrix products, arithmetic and copies ran while one was open for 0% of the time, Pallas kernels for 14%

profile of v3, /device:TPU:17, one launch (start us, length us, event | category | flops | bytes accessed | tf_op | source)
XLA Modules:
  0.0 40.9 jit_solution(6566814373226993908)
XLA Ops:
  0.0 1.7 %pack.1 = (bf16[64,1152]{1,0:T(8,128)(2,1)S(1)}, bf16[64,1152]{1,0:T(8,128)(2,1)S(1)}, bf16[64,1152]{1,0:T(8,128)(2,1)S(1)}, bf16[64,1152]{1,0:T(8,128)(2,1)S(1)...) custom-call(s32[16]{0:T(128)} %assign_hbm.1, ...), custom_call_target="tpu_custom_call" | custom-call | tf_op jit(solution)/shard_map/pack/pallas_call | solution.py:81
  1.7 0.7 %collective-permute-start.14 = (bf16[64,1152]{1,0:T(8,128)(2,1)S(1)}, bf16[64,1152]{1,0:T(8,128)(2,1)S(1)}, u32[]{:S(2)}, u32[]{:S(2)}) collective-permute-start(bf16[64,1152]{1,0:T(8,128)(2,1)S(1)} %get-tuple-element.34.refs_0_), channel_id=1, source_target_pairs={{0,1},{1,0},{2,3},{3,2},{4,5},{5,4},{6,7},{7,6},{8,9},{9,8},{10,11... | collective-permute-start | bytes 442376 | tf_op jit(solution)/shard_map/ppermute | solution.py:313
  2.4 3.3 %collective-permute-start.11 = (bf16[64,1152]{1,0:T(8,128)(2,1)S(1)}, bf16[64,1152]{1,0:T(8,128)(2,1)S(1)}, u32[]{:S(2)}, u32[]{:S(2)}) collective-permute-start(bf16[64,1152]{1,0:T(8,128)(2,1)S(1)} %get-tuple-element.33), channel_id=1, source_target_pairs={{0,10},{2,8},{4,14},{6,12},{8,2},{10,0},{12,6},{14,4},{1,11},{3,9}... | collective-permute-start | bytes 442376 | tf_op jit(solution)/shard_map/ppermute | solution.py:305
  5.7 0.2 collective-permute-start.2
  6.0 1.3 %collective-permute-start.3 = (bf16[64,1152]{1,0:T(8,128)(2,1)S(1)}, bf16[64,1152]{1,0:T(8,128)(2,1)S(1)}, u32[]{:S(2)}, u32[]{:S(2)}) collective-permute-start(bf16[64,1152]{1,0:T(8,128)(2,1)S(1)} %get-tuple-element.29), channel_id=1, source_target_pairs={{0,4},{2,6},{4,0},{6,2},{8,12},{10,14},{12,8},{14,10},{1,5},{3,7},... | collective-permute-start | bytes 442376 | tf_op jit(solution)/shard_map/ppermute | solution.py:305
  7.3 1.1 %collective-permute-start.4 = (bf16[64,1152]{1,0:T(8,128)(2,1)S(1)}, bf16[64,1152]{1,0:T(8,128)(2,1)S(1)}, u32[]{:S(2)}, u32[]{:S(2)}) collective-permute-start(bf16[64,1152]{1,0:T(8,128)(2,1)S(1)} %get-tuple-element.30), channel_id=1, source_target_pairs={{0,6},{2,4},{4,2},{6,0},{8,14},{10,12},{12,10},{14,8},{1,7},{3,5},... | collective-permute-start | bytes 442376 | tf_op jit(solution)/shard_map/ppermute | solution.py:305
  8.4 3.8 %collective-permute-done.10.refs_0_ = bf16[64,1152]{1,0:T(8,128)(2,1)S(1)} collective-permute-done((bf16[64,1152]{1,0:T(8,128)(2,1)S(1)}, bf16[64,1152]{1,0:T(8,128)(2,1)S(1)}, u32[]{:S(2)}, u32[]{:S(2)}) %collective-permute-start.10) | collective-permute-done | bytes 147488 | tf_op jit(solution)/shard_map/ppermute | solution.py:305
  12.1 2.6 %collective-permute-start.5 = (bf16[64,1152]{1,0:T(8,128)(2,1)S(1)}, bf16[64,1152]{1,0:T(8,128)(2,1)S(1)}, u32[]{:S(2)}, u32[]{:S(2)}) collective-permute-start(bf16[64,1152]{1,0:T(8,128)(2,1)S(1)} %get-tuple-element.31), channel_id=1, source_target_pairs={{0,12},{2,14},{4,8},{6,10},{8,4},{10,6},{12,0},{14,2},{1,13},{3,15... | collective-permute-start | bytes 442376 | tf_op jit(solution)/shard_map/ppermute | solution.py:305
  14.8 0.6 %collective-permute-done.11.refs_1_ = bf16[64,1152]{1,0:T(8,128)(2,1)S(1)} collective-permute-done((bf16[64,1152]{1,0:T(8,128)(2,1)S(1)}, bf16[64,1152]{1,0:T(8,128)(2,1)S(1)}, u32[]{:S(2)}, u32[]{:S(2)}) %collective-permute-start.11) | collective-permute-done | bytes 147488 | tf_op jit(solution)/shard_map/ppermute | solution.py:305
  15.3 3.5 %collective-permute-start = (bf16[64,1152]{1,0:T(8,128)(2,1)S(1)}, bf16[64,1152]{1,0:T(8,128)(2,1)S(1)}, u32[]{:S(2)}, u32[]{:S(2)}) collective-permute-start(bf16[64,1152]{1,0:T(8,128)(2,1)S(1)} %get-tuple-element.27), channel_id=1, source_target_pairs={{0,14},{2,12},{4,10},{6,8},{8,6},{10,4},{12,2},{14,0},{1,15},{3,13... | collective-permute-start | bytes 442376 | tf_op jit(solution)/shard_map/ppermute | solution.py:305
  18.9 0.8 %collective-permute-start.12 = (bf16[64,1152]{1,0:T(8,128)(2,1)S(1)}, bf16[64,1152]{1,0:T(8,128)(2,1)S(1)}, u32[]{:S(2)}, u32[]{:S(2)}) collective-permute-start(bf16[64,1152]{1,0:T(8,128)(2,1)S(1)} %collective-permute-done.10.refs_0_), channel_id=1, source_target_pairs={{0,1},{1,0},{2,3},{3,2},{4,5},{5,4},{6,7},{7,6},{8,9},{9,8},{10,11... | collective-permute-start | bytes 442376 | tf_op jit(solution)/shard_map/ppermute | solution.py:313
  19.6 0.1 collective-permute-start.13
  19.7 7.3 %collective-permute-start.6 = (bf16[64,1152]{1,0:T(8,128)(2,1)S(1)}, bf16[64,1152]{1,0:T(8,128)(2,1)S(1)}, u32[]{:S(2)}, u32[]{:S(2)}) collective-permute-start(bf16[64,1152]{1,0:T(8,128)(2,1)S(1)} %collective-permute-done.2.refs_0_), channel_id=1, source_target_pairs={{0,1},{1,0},{2,3},{3,2},{4,5},{5,4},{6,7},{7,6},{8,9},{9,8},{10,11... | collective-permute-start | bytes 442376 | tf_op jit(solution)/shard_map/ppermute | solution.py:313
  27.0 1.1 %collective-permute-done.5.refs_3_ = bf16[64,1152]{1,0:T(8,128)(2,1)S(1)} collective-permute-done((bf16[64,1152]{1,0:T(8,128)(2,1)S(1)}, bf16[64,1152]{1,0:T(8,128)(2,1)S(1)}, u32[]{:S(2)}, u32[]{:S(2)}) %collective-permute-start.5) | collective-permute-done | bytes 147488 | tf_op jit(solution)/shard_map/ppermute | solution.py:305
  28.1 0.5 %collective-permute-start.7 = (bf16[64,1152]{1,0:T(8,128)(2,1)S(1)}, bf16[64,1152]{1,0:T(8,128)(2,1)S(1)}, u32[]{:S(2)}, u32[]{:S(2)}) collective-permute-start(bf16[64,1152]{1,0:T(8,128)(2,1)S(1)} %collective-permute-done.3.refs_1_), channel_id=1, source_target_pairs={{0,1},{1,0},{2,3},{3,2},{4,5},{5,4},{6,7},{7,6},{8,9},{9,8},{10,11... | collective-permute-start | bytes 442376 | tf_op jit(solution)/shard_map/ppermute | solution.py:313
  28.6 3.6 %collective-permute-done.refs_0_ = bf16[64,1152]{1,0:T(8,128)(2,1)S(1)} collective-permute-done((bf16[64,1152]{1,0:T(8,128)(2,1)S(1)}, bf16[64,1152]{1,0:T(8,128)(2,1)S(1)}, u32[]{:S(2)}, u32[]{:S(2)}) %collective-permute-start) | collective-permute-done | bytes 147488 | tf_op jit(solution)/shard_map/ppermute | solution.py:305
  32.2 0.4 %collective-permute-start.8 = (bf16[64,1152]{1,0:T(8,128)(2,1)S(1)}, bf16[64,1152]{1,0:T(8,128)(2,1)S(1)}, u32[]{:S(2)}, u32[]{:S(2)}) collective-permute-start(bf16[64,1152]{1,0:T(8,128)(2,1)S(1)} %collective-permute-done.4.refs_2_), channel_id=1, source_target_pairs={{0,1},{1,0},{2,3},{3,2},{4,5},{5,4},{6,7},{7,6},{8,9},{9,8},{10,11... | collective-permute-start | bytes 442376 | tf_op jit(solution)/shard_map/ppermute | solution.py:313
  32.7 0.1 collective-permute-start.9
  32.8 0.4 %collective-permute-start.1 = (bf16[64,1152]{1,0:T(8,128)(2,1)S(1)}, bf16[64,1152]{1,0:T(8,128)(2,1)S(1)}, u32[]{:S(2)}, u32[]{:S(2)}) collective-permute-start(bf16[64,1152]{1,0:T(8,128)(2,1)S(1)} %collective-permute-done.refs_0_), channel_id=1, source_target_pairs={{0,1},{1,0},{2,3},{3,2},{4,5},{5,4},{6,7},{7,6},{8,9},{9,8},{10,11... | collective-permute-start | bytes 442376 | tf_op jit(solution)/shard_map/ppermute | solution.py:313
  33.2 1.3 %spread.1 = (bf16[2,256,640]{2,1,0:T(8,128)(2,1)S(1)}, bf16[2,576,256]{2,1,0:T(8,128)(2,1)S(1)}) custom-call(bf16[4,2,64,576]{3,2,1,0:T(8,128)(2,1)} %q_hbm.1, bf16[2,576,256]{2,1,0:T(8,128)(2,1)} %bitcast.7), custom_call_target="tpu_custom_call" | custom-call | tf_op jit(solution)/shard_map/spread/pallas_call | solution.py:124
  34.5 1.6 %attend.3 = (f32[2,256,1]{2,1,0:T(8,128)S(1)}, f32[2,256,1]{2,1,0:T(8,128)S(1)}, f32[2,256,512]{2,1,0:T(8,128)S(1)}) custom-call(f32[2,1280]{1,0:T(2,128)S(1)} %get-tuple-element.25.bias_ref, bf16[2,256,640]{2,1,0:T(8,128)(2,1)S(1)} %get-tuple-element.26.q_ref, bf16[64,1152]{1,0:T(8,128)(2,1)S(1)} %get-tuple-element.34.refs_0_, ...), custom_call_target="tpu_custom_call" | custom-call | flops 150994944 | bytes 983040 | tf_op jit(solution)/shard_map/attend/pallas_call | solution.py:231
  36.1 1.4 %attend.4 = (f32[2,256,1]{2,1,0:T(8,128)S(1)}, f32[2,256,1]{2,1,0:T(8,128)S(1)}, f32[2,256,512]{2,1,0:T(8,128)S(1)}) custom-call(f32[2,1280]{1,0:T(2,128)S(1)} %get-tuple-element.25.bias_ref, bf16[2,256,640]{2,1,0:T(8,128)(2,1)S(1)} %get-tuple-element.26.q_ref, bf16[64,1152]{1,0:T(8,128)(2,1)S(1)} %collective-permute-done.10.refs_0_, ...), custom_call_target="tpu_custom_call" | custom-call | flops 301989888 | bytes 1310720 | tf_op jit(solution)/shard_map/attend/pallas_call | solution.py:231
  37.6 1.5 %attend.5 = (f32[2,256,1]{2,1,0:T(8,128)S(1)}, f32[2,256,1]{2,1,0:T(8,128)S(1)}, f32[2,256,512]{2,1,0:T(8,128)S(1)}) custom-call(f32[2,1280]{1,0:T(2,128)S(1)} %get-tuple-element.25.bias_ref, bf16[2,256,640]{2,1,0:T(8,128)(2,1)S(1)} %get-tuple-element.26.q_ref, bf16[64,1152]{1,0:T(8,128)(2,1)S(1)} %collective-permute-done.2.refs_0_, ...), custom_call_target="tpu_custom_call" | custom-call | flops 603979776 | bytes 1966080 | tf_op jit(solution)/shard_map/attend/pallas_call | solution.py:231
  39.1 1.8 %attend_last.1 = bf16[4,2,64,512]{3,2,1,0:T(8,128)(2,1)} custom-call(f32[2,1280]{1,0:T(2,128)S(1)} %get-tuple-element.25.bias_ref, bf16[2,256,640]{2,1,0:T(8,128)(2,1)S(1)} %get-tuple-element.26.q_ref, bf16[64,1152]{1,0:T(8,128)(2,1)S(1)} %collective-permute-done.refs_0_, bf16[64,1152]{1,0:T(8,128)(2,1)S(1)} %collective-permute-done.1.refs_1_, ...), custom_call_target="tpu_custom_call" | custom-call | flops 150994944 | bytes 983040 | tf_op jit(solution)/shard_map/attend_last/pallas_call | solution.py:231
  (15 shorter events, 0.0 us)
Async XLA Ops:
  0.0 33.2 %copy-start = (bf16[4,2,576]{2,1,0:T(2,128)(2,1)S(1)}, bf16[4,2,576]{2,1,0:T(2,128)(2,1)}, u32[]{:S(2)}) copy-start(bf16[4,2,576]{2,1,0:T(2,128)(2,1)} %param.10) | copy-start | bytes 27652
  1.7 5.6 %collective-permute-start.14 = (bf16[64,1152]{1,0:T(8,128)(2,1)S(1)}, bf16[64,1152]{1,0:T(8,128)(2,1)S(1)}, u32[]{:S(2)}, u32[]{:S(2)}) collective-permute-start(bf16[64,1152]{1,0:T(8,128)(2,1)S(1)} %get-tuple-element.34.refs_0_), channel_id=1, source_target_pairs={{0,1},{1,0},{2,3},{3,2},{4,5},{5,4},{6,7},{7,6},{8,9},{9,8},{10,11... | collective-permute-start | bytes 442376 | tf_op jit(solution)/shard_map/ppermute | solution.py:313
  2.4 9.7 %collective-permute-start.10 = (bf16[64,1152]{1,0:T(8,128)(2,1)S(1)}, bf16[64,1152]{1,0:T(8,128)(2,1)S(1)}, u32[]{:S(2)}, u32[]{:S(2)}) collective-permute-start(bf16[64,1152]{1,0:T(8,128)(2,1)S(1)} %get-tuple-element.32), channel_id=1, source_target_pairs={{0,8},{2,10},{4,12},{6,14},{8,0},{10,2},{12,4},{14,6},{1,9},{3,11}... | collective-permute-start | bytes 442376 | tf_op jit(solution)/shard_map/ppermute | solution.py:305
  2.4 12.9 %collective-permute-start.11 = (bf16[64,1152]{1,0:T(8,128)(2,1)S(1)}, bf16[64,1152]{1,0:T(8,128)(2,1)S(1)}, u32[]{:S(2)}, u32[]{:S(2)}) collective-permute-start(bf16[64,1152]{1,0:T(8,128)(2,1)S(1)} %get-tuple-element.33), channel_id=1, source_target_pairs={{0,10},{2,8},{4,14},{6,12},{8,2},{10,0},{12,6},{14,4},{1,11},{3,9}... | collective-permute-start | bytes 442376 | tf_op jit(solution)/shard_map/ppermute | solution.py:305
  5.7 13.1 %collective-permute-start.2 = (bf16[64,1152]{1,0:T(8,128)(2,1)S(1)}, bf16[64,1152]{1,0:T(8,128)(2,1)S(1)}, u32[]{:S(2)}, u32[]{:S(2)}) collective-permute-start(bf16[64,1152]{1,0:T(8,128)(2,1)S(1)} %get-tuple-element.28), channel_id=1, source_target_pairs={{0,2},{2,0},{4,6},{6,4},{8,10},{10,8},{12,14},{14,12},{1,3},{3,1},... | collective-permute-start | bytes 442376 | tf_op jit(solution)/shard_map/ppermute | solution.py:305
  6.0 13.7 %collective-permute-start.3 = (bf16[64,1152]{1,0:T(8,128)(2,1)S(1)}, bf16[64,1152]{1,0:T(8,128)(2,1)S(1)}, u32[]{:S(2)}, u32[]{:S(2)}) collective-permute-start(bf16[64,1152]{1,0:T(8,128)(2,1)S(1)} %get-tuple-element.29), channel_id=1, source_target_pairs={{0,4},{2,6},{4,0},{6,2},{8,12},{10,14},{12,8},{14,10},{1,5},{3,7},... | collective-permute-start | bytes 442376 | tf_op jit(solution)/shard_map/ppermute | solution.py:305
  7.3 12.5 %collective-permute-start.4 = (bf16[64,1152]{1,0:T(8,128)(2,1)S(1)}, bf16[64,1152]{1,0:T(8,128)(2,1)S(1)}, u32[]{:S(2)}, u32[]{:S(2)}) collective-permute-start(bf16[64,1152]{1,0:T(8,128)(2,1)S(1)} %get-tuple-element.30), channel_id=1, source_target_pairs={{0,6},{2,4},{4,2},{6,0},{8,14},{10,12},{12,10},{14,8},{1,7},{3,5},... | collective-permute-start | bytes 442376 | tf_op jit(solution)/shard_map/ppermute | solution.py:305
  12.1 16.0 %collective-permute-start.5 = (bf16[64,1152]{1,0:T(8,128)(2,1)S(1)}, bf16[64,1152]{1,0:T(8,128)(2,1)S(1)}, u32[]{:S(2)}, u32[]{:S(2)}) collective-permute-start(bf16[64,1152]{1,0:T(8,128)(2,1)S(1)} %get-tuple-element.31), channel_id=1, source_target_pairs={{0,12},{2,14},{4,8},{6,10},{8,4},{10,6},{12,0},{14,2},{1,13},{3,15... | collective-permute-start | bytes 442376 | tf_op jit(solution)/shard_map/ppermute | solution.py:305
  15.3 16.9 %collective-permute-start = (bf16[64,1152]{1,0:T(8,128)(2,1)S(1)}, bf16[64,1152]{1,0:T(8,128)(2,1)S(1)}, u32[]{:S(2)}, u32[]{:S(2)}) collective-permute-start(bf16[64,1152]{1,0:T(8,128)(2,1)S(1)} %get-tuple-element.27), channel_id=1, source_target_pairs={{0,14},{2,12},{4,10},{6,8},{8,6},{10,4},{12,2},{14,0},{1,15},{3,13... | collective-permute-start | bytes 442376 | tf_op jit(solution)/shard_map/ppermute | solution.py:305
  18.9 13.8 %collective-permute-start.12 = (bf16[64,1152]{1,0:T(8,128)(2,1)S(1)}, bf16[64,1152]{1,0:T(8,128)(2,1)S(1)}, u32[]{:S(2)}, u32[]{:S(2)}) collective-permute-start(bf16[64,1152]{1,0:T(8,128)(2,1)S(1)} %collective-permute-done.10.refs_0_), channel_id=1, source_target_pairs={{0,1},{1,0},{2,3},{3,2},{4,5},{5,4},{6,7},{7,6},{8,9},{9,8},{10,11... | collective-permute-start | bytes 442376 | tf_op jit(solution)/shard_map/ppermute | solution.py:313
  19.6 13.1 %collective-permute-start.13 = (bf16[64,1152]{1,0:T(8,128)(2,1)S(1)}, bf16[64,1152]{1,0:T(8,128)(2,1)S(1)}, u32[]{:S(2)}, u32[]{:S(2)}) collective-permute-start(bf16[64,1152]{1,0:T(8,128)(2,1)S(1)} %collective-permute-done.11.refs_1_), channel_id=1, source_target_pairs={{0,1},{1,0},{2,3},{3,2},{4,5},{5,4},{6,7},{7,6},{8,9},{9,8},{10,11... | collective-permute-start | bytes 442376 | tf_op jit(solution)/shard_map/ppermute | solution.py:313
  19.7 17.8 %collective-permute-start.6 = (bf16[64,1152]{1,0:T(8,128)(2,1)S(1)}, bf16[64,1152]{1,0:T(8,128)(2,1)S(1)}, u32[]{:S(2)}, u32[]{:S(2)}) collective-permute-start(bf16[64,1152]{1,0:T(8,128)(2,1)S(1)} %collective-permute-done.2.refs_0_), channel_id=1, source_target_pairs={{0,1},{1,0},{2,3},{3,2},{4,5},{5,4},{6,7},{7,6},{8,9},{9,8},{10,11... | collective-permute-start | bytes 442376 | tf_op jit(solution)/shard_map/ppermute | solution.py:313
  28.1 9.4 %collective-permute-start.7 = (bf16[64,1152]{1,0:T(8,128)(2,1)S(1)}, bf16[64,1152]{1,0:T(8,128)(2,1)S(1)}, u32[]{:S(2)}, u32[]{:S(2)}) collective-permute-start(bf16[64,1152]{1,0:T(8,128)(2,1)S(1)} %collective-permute-done.3.refs_1_), channel_id=1, source_target_pairs={{0,1},{1,0},{2,3},{3,2},{4,5},{5,4},{6,7},{7,6},{8,9},{9,8},{10,11... | collective-permute-start | bytes 442376 | tf_op jit(solution)/shard_map/ppermute | solution.py:313
  32.2 5.3 %collective-permute-start.8 = (bf16[64,1152]{1,0:T(8,128)(2,1)S(1)}, bf16[64,1152]{1,0:T(8,128)(2,1)S(1)}, u32[]{:S(2)}, u32[]{:S(2)}) collective-permute-start(bf16[64,1152]{1,0:T(8,128)(2,1)S(1)} %collective-permute-done.4.refs_2_), channel_id=1, source_target_pairs={{0,1},{1,0},{2,3},{3,2},{4,5},{5,4},{6,7},{7,6},{8,9},{9,8},{10,11... | collective-permute-start | bytes 442376 | tf_op jit(solution)/shard_map/ppermute | solution.py:313
  32.7 4.9 %collective-permute-start.9 = (bf16[64,1152]{1,0:T(8,128)(2,1)S(1)}, bf16[64,1152]{1,0:T(8,128)(2,1)S(1)}, u32[]{:S(2)}, u32[]{:S(2)}) collective-permute-start(bf16[64,1152]{1,0:T(8,128)(2,1)S(1)} %collective-permute-done.5.refs_3_), channel_id=1, source_target_pairs={{0,1},{1,0},{2,3},{3,2},{4,5},{5,4},{6,7},{7,6},{8,9},{9,8},{10,11... | collective-permute-start | bytes 442376 | tf_op jit(solution)/shard_map/ppermute | solution.py:313
  32.8 6.4 %collective-permute-start.1 = (bf16[64,1152]{1,0:T(8,128)(2,1)S(1)}, bf16[64,1152]{1,0:T(8,128)(2,1)S(1)}, u32[]{:S(2)}, u32[]{:S(2)}) collective-permute-start(bf16[64,1152]{1,0:T(8,128)(2,1)S(1)} %collective-permute-done.refs_0_), channel_id=1, source_target_pairs={{0,1},{1,0},{2,3},{3,2},{4,5},{5,4},{6,7},{7,6},{8,9},{9,8},{10,11... | collective-permute-start | bytes 442376 | tf_op jit(solution)/shard_map/ppermute | solution.py:313
